TPU v7x, 32 devices: a whole 2x2x4 slice. The times are simulated.
32 devices in a mesh: section: 4 (over y, core), dp: 8 (over z, x).
Axes of the slice: x: 2, y: 2, z: 4, core: 2. Of those that a mesh axis runs over, the one named last changes fastest.
Arguments:
- fresh_batches: bfloat16 [3, 512, 4096], P(None, 'dp'), may hold values from -6 to 6
- held_states: bfloat16 [4, 512, 4096], P('section', 'dp'), may hold values from -6 to 6
- section_weight: bfloat16 [4, 4096, 4096], P('section', None, 'dp'), may hold values from -0.09375 to 0.09375
- section_gain: float32 [4, 4096], P('section'), may hold values from 0.25 to 1.75
- final_gain: float32 [4096], replicated, may hold values from 0.3 to 3
- cached_pool: bfloat16 [512, 4096], P('dp'), may hold values from -0.09375 to 0.09375
- route: int32 [8, 64], P('dp'), may hold values from 0 to 63, each once within a row
- queries: bfloat16 [256, 4096], P(('section', 'dp')), may hold values from -0.09375 to 0.09375
- shortlist: int32 [256, 128], P(('section', 'dp')), may hold values from 0 to 63
- teacher: float32 [256, 128], P(('section', 'dp')), may hold values from -16 to 300, as said below
Outputs:
- held_out: bfloat16 [4, 512, 4096], P('section', 'dp')
- losses: float32 [256], P(('section', 'dp'))
- query_grad: float32 [256, 4096], P(('section', 'dp'))
- pool_grad: bfloat16 [512, 4096], P('dp')
Inputs may be any that keep to these rules, and one draw needn't show every extreme that they name: `teacher`: reranker scores; on some draws some rows have two entries above the rest.
All inputs are finite; a program needn't handle non-finite values.
Results may differ from a plain program's by a relative error of at most 0.0058.
Values may be sent and summed in bfloat16 or wider, within the bound.
No kernel may reach another device: no remote copies, remote signals or barrier semaphores. Data moves between devices by JAX's collectives and lax.ppermute only.
A program may use at most 64 MiB of HBM per device.

v0:
```python
import functools

import jax
import jax.numpy as jnp
from jax import lax
from jax.experimental import pallas as pl
from jax.experimental.pallas import tpu as pltpu
from jax.sharding import PartitionSpec as P


SEQ = 128
TICKS = 3


epsilon = 1e-06
logit_scale = 20.0

AXES = ("section", "dp")


LANES = 128


def gain_kernel(at_ref, weight_ref, gain_ref, out_ref):
    cols = gain_ref.shape[-1]
    column = jnp.transpose(jnp.broadcast_to(gain_ref[0], (LANES, cols)))[:, :1]
    out_ref[...] = (weight_ref[...].astype(jnp.float32) * column).astype(jnp.bfloat16)


def gained_blocks(weight, gain, at):
    cols = weight.shape[1]
    count = at.shape[0]
    return pl.pallas_call(
        gain_kernel,
        out_shape=jax.ShapeDtypeStruct((count * cols, cols), jnp.bfloat16),
        grid_spec=pltpu.PrefetchScalarGridSpec(
            num_scalar_prefetch=1,
            grid=(count,),
            in_specs=[
                pl.BlockSpec((cols, cols), lambda k, at: (at[k], 0)),
                pl.BlockSpec((1, 1, cols), lambda k, at: (at[k], 0, 0)),
            ],
            out_specs=pl.BlockSpec((cols, cols), lambda k, at: (k, 0)),
        ),
        cost_estimate=pl.CostEstimate(
            flops=count * cols * cols, bytes_accessed=4 * count * cols * cols, transcendentals=0
        ),
    )(at, weight, gain.reshape(-1, 1, cols))


def sent_kernel(half, at_ref, *refs):
    *piles, weight_ref, out_ref, square_ref, states_ref = refs
    row_piles, column_piles = piles[:half], piles[half:]
    tile = row_piles[0].shape[0]
    cols = weight_ref.shape[1]

    def by_rows():
        for k, pile in enumerate(row_piles):
            states_ref[k * tile : (k + 1) * tile, :] = pile[...]

    def by_columns():
        for k, pile in enumerate(column_piles):
            states_ref[:, k * cols : (k + 1) * cols] = pile[...]

    if column_piles:
        pl.when(at_ref[0] == 1)(by_rows)
        pl.when(at_ref[0] != 1)(by_columns)
    else:
        by_rows()
    tokens = states_ref.shape[0]
    out_ref[:, :cols] = jnp.dot(
        states_ref[...], weight_ref[...], preferred_element_type=jnp.float32
    ).astype(jnp.bfloat16)
    wide = states_ref[...].astype(jnp.float32)
    square = jnp.sum(wide * wide, axis=-1, keepdims=True)
    high = square.astype(jnp.bfloat16).astype(jnp.float32)
    middle = (square - high).astype(jnp.bfloat16).astype(jnp.float32)
    low = square - high - middle
    lane = lax.broadcasted_iota(jnp.int32, (tokens, LANES), 1)
    terms = jnp.where(lane == 0, high, jnp.where(lane == 1, middle, jnp.where(lane == 2, low, 0.0)))
    out_ref[:, cols:] = terms.astype(jnp.bfloat16)
    square_ref[...] = jnp.broadcast_to(square, (tokens, LANES))


def kept_kernel(width, tile, at_ref, states_ref, weight_ref, other_ref, square_ref, out_ref):
    tokens, cols = out_ref.shape
    own = jnp.dot(states_ref[...], weight_ref[...], preferred_element_type=jnp.float32)
    total = own + other_ref[:, :cols].astype(jnp.float32)
    square = square_ref[:, :1] + jnp.sum(
        other_ref[:, cols:].astype(jnp.float32), axis=-1, keepdims=True
    )
    projected = (total * lax.rsqrt(square / width + epsilon)).astype(jnp.bfloat16)
    kept = states_ref[:, pl.ds(pl.multiple_of(at_ref[1] * cols, LANES), cols)]
    result = (
        kept.astype(jnp.float32) + jax.nn.silu(projected.astype(jnp.float32))
    ).astype(jnp.bfloat16)
    for i in range(tokens // tile):
        spot = pl.multiple_of((i ^ at_ref[2]) * tile, tile)
        out_ref[pl.ds(spot, tile), :] = result[i * tile : (i + 1) * tile]


def specs(count):
    vmem = pl.BlockSpec(memory_space=pltpu.VMEM)
    return [pl.BlockSpec(memory_space=pltpu.SMEM)] + [vmem] * count


def cost(tokens, inner, cols):
    return pl.CostEstimate(
        flops=2 * tokens * inner * cols,
        bytes_accessed=2 * inner * (tokens + cols),
        transcendentals=0,
    )


PARAMS = pltpu.CompilerParams(vmem_limit_bytes=24 << 20)


def sent_half(at, row_piles, column_piles, weight):
    inner, cols = weight.shape
    tokens = len(row_piles) * row_piles[0].shape[0]
    return pl.pallas_call(
        functools.partial(sent_kernel, len(row_piles)),
        out_shape=(
            jax.ShapeDtypeStruct((tokens, cols + LANES), jnp.bfloat16),
            jax.ShapeDtypeStruct((tokens, LANES), jnp.float32),
            jax.ShapeDtypeStruct((tokens, inner), jnp.bfloat16),
        ),
        in_specs=specs(len(row_piles) + len(column_piles) + 1),
        out_specs=(pl.BlockSpec(memory_space=pltpu.VMEM),) * 3,
        compiler_params=PARAMS,
        cost_estimate=cost(tokens, inner, cols),
    )(at, *row_piles, *column_piles, weight)


def kept_half(at, states, weight, other, square, width, tile):
    inner, cols = weight.shape
    tokens = states.shape[0]
    return pl.pallas_call(
        functools.partial(kept_kernel, width, tile),
        out_shape=jax.ShapeDtypeStruct((tokens, cols), jnp.bfloat16),
        in_specs=specs(4),
        out_specs=pl.BlockSpec(memory_space=pltpu.VMEM),
        compiler_params=PARAMS,
        cost_estimate=cost(tokens, inner, cols),
    )(at, states, weight, other, square)


def on_device(
    fresh_batches,
    held_states,
    section_weight,
    section_gain,
    final_gain,
    cached_pool,
    route,
    queries,
    shortlist,
    teacher,
):
    section = lax.axis_index("section")
    sections = lax.axis_size("section")
    dp = lax.axis_index("dp")
    dps = lax.axis_size("dp")
    half = dps // 2
    side, place = dp % 2, dp // 2
    weight = section_weight[0]
    gain = section_gain[0]
    width, cols = weight.shape
    tok = held_states.shape[1]
    pair_rows = 2 * tok

    def send(x, hops):
        return lax.ppermute(
            x, AXES, [(a * dps + i, b * dps + (i ^ flip)) for a, b, flip in hops for i in range(dps)]
        )

    def rows_at(x, index):
        return x.at[index].get(mode="promise_in_bounds")

    flips = jnp.where(section == 0, 0, place)
    last_full = sections - 1 - TICKS

    def split_weights(order, firsts):
        theirs = gained_blocks(weight, gain, 2 * order + 1 - side)
        mine = gained_blocks(weight, gain, 2 * order + side)
        rest = [a for a in range(sections - 1) if a not in firsts]
        came = send(theirs, [(a, a, 1) for a in firsts])
        if rest:
            later = send(theirs, [(a, a, 1) for a in rest])
        else:
            later = came
        return mine, came, jnp.where(section <= max(firsts), came, later)

    mine_late, theirs_first, theirs_late = split_weights(
        jnp.arange(half) ^ flips, list(range(last_full + 1))
    )
    mine_first = mine_late
    if last_full > 0:
        mine_first, _, theirs_first = split_weights(
            jnp.arange(half), list(range(last_full + 1))
        )

    used = list(range(last_full + 1))

    def sides(x):
        pieces = [x[:, k * cols : (k + 1) * cols] for k in range(dps)]
        even, odd = jnp.concatenate(pieces[0::2], axis=1), jnp.concatenate(pieces[1::2], axis=1)
        return jnp.where(side == 0, even, odd), jnp.where(side == 0, odd, even)

    entries = jnp.concatenate([held_states[0], *fresh_batches[: TICKS - 1]], axis=0)
    stay, leave = sides(entries)
    came = send(leave, [(a, a, 1) for a in used])

    def gathered(i, owners):
        here, there = stay[i * tok : (i + 1) * tok], came[i * tok : (i + 1) * tok]
        pair = jnp.where(
            side == 0,
            jnp.concatenate([here, there], axis=0),
            jnp.concatenate([there, here], axis=0),
        )
        return [pair] + [send(pair, [(a, a, 2 * k) for a in owners]) for k in range(1, half)]

    entry_piles = gathered(0, used)
    fresh_piles = []
    for i in range(TICKS - 1):
        fresh_piles.append(gathered(i + 1, [0]))

    rows = cached_pool.shape[0]
    per_peer = rows // dps
    last_token = held_states[0, tok - 1].reshape(1, per_peer, width // per_peer)
    outbox = jnp.concatenate(
        [
            rows_at(cached_pool, route[0]).reshape(dps, per_peer, width),
            jnp.broadcast_to(last_token, (dps, per_peer, width // per_peer)),
            jnp.broadcast_to(
                route[0].astype(jnp.bfloat16).reshape(dps, per_peer, 1), (dps, per_peer, 128)
            ),
        ],
        axis=2,
    )
    inbox = lax.all_to_all(outbox, "dp", split_axis=0, concat_axis=0)
    owner_queries = lax.all_gather(queries, "section", axis=0, tiled=True)

    def layer(row_piles, column_piles, mine, theirs, at, hops):
        at = jnp.stack([jnp.asarray(x, jnp.int32) for x in at])
        part, square, states = sent_half(at, row_piles, column_piles, theirs)
        other = send(part, hops)
        return kept_half(at, states, mine, other, square, width, pair_rows)

    block = layer(
        entry_piles,
        [],
        mine_first,
        theirs_first,
        (1, place, place),
        [(a, a, 1) for a in range(last_full + 1)],
    )
    first = section == 0
    row_order = jnp.where(first, place, 0)
    for tick in range(1, TICKS):
        top = last_full + tick
        if tick == 1:
            piles = [
                send(block, [(a - 1, a, 2 * k) for a in range(1, top + 1)])
                for k in range(half)
            ]
        else:
            block = send(block, [(a - 1, a, 0) for a in range(1, top + 1)])
            piles = [block] + [
                send(block, [(a, a, 2 * k) for a in range(1, top + 1)])
                for k in range(1, half)
            ]
        block = layer(
            fresh_piles[tick - 1],
            piles,
            mine_late,
            theirs_late,
            (first, row_order, row_order),
            [(a, a, 1) for a in range(top + 1)],
        )
    tokens = lax.all_to_all(block, "dp", split_axis=0, concat_axis=1, tiled=True)
    shifted = send(tokens, [(a, a + 1, 0) for a in range(sections - 1)])
    held_out = jnp.where(section == 0, fresh_batches[TICKS - 1], shifted)[None]

    def spread(x):
        pieces = lax.all_to_all(
            jnp.broadcast_to(x[None], (dps, *x.shape)), "dp", split_axis=0, concat_axis=0
        )
        return jnp.transpose(pieces, (1, 0, 2)).reshape(x.shape[0], width)

    every = SEQ // tok
    ends = inbox[every - 1 :: every, :, width : width + width // per_peer].reshape(-1, width)
    exits = []
    for tick in range(TICKS):
        wide = ends.astype(jnp.float32)
        inv_rms = lax.rsqrt(jnp.mean(wide * wide, axis=-1, keepdims=True) + epsilon)
        normed = (wide * inv_rms * gain).astype(jnp.bfloat16)
        projected = jnp.dot(normed, weight, preferred_element_type=jnp.float32)
        projected = projected.astype(jnp.bfloat16).astype(jnp.float32)
        kept = lax.dynamic_slice_in_dim(wide, dp * cols, cols, axis=1)
        piece = (kept + jax.nn.silu(projected)).astype(jnp.bfloat16)
        exits.append(piece)
        if tick < TICKS - 1:
            piece = send(
                piece, [(a, a + 1, 0) for a in range(sections - TICKS + tick, sections - 1)]
            )
            ends = spread(piece)
    passages = ends.shape[0]
    exit_pieces = lax.all_gather(jnp.concatenate(exits, axis=0), "section", axis=0)
    exit_rows = spread(exit_pieces[sections - 1])
    scaled = exit_rows.astype(jnp.float32) * final_gain
    embedded = (
        scaled * lax.rsqrt(jnp.sum(scaled * scaled, axis=-1, keepdims=True) + epsilon)
    ).astype(jnp.bfloat16)

    source = jnp.arange(rows) // per_peer
    passage = source // every
    is_end = source % every == every - 1
    slot = inbox[:, :, width + width // per_peer].reshape(rows).astype(jnp.int32)
    replaced = is_end & (slot < TICKS)
    pick = jnp.where(replaced, slot * passages + passage, -1)
    chosen = (pick[:, None] == jnp.arange(TICKS * passages)).astype(jnp.bfloat16)
    received = jnp.where(
        replaced[:, None],
        jnp.dot(chosen, embedded, preferred_element_type=jnp.float32).astype(jnp.bfloat16),
        inbox[:, :, :width].reshape(rows, width),
    )
    all_scores = lax.dot_general(
        queries, received, (((1,), (1,)), ((), ())), preferred_element_type=jnp.float32
    )
    listed = shortlist[..., None] == jnp.arange(rows, dtype=jnp.int32)
    student = jnp.sum(jnp.where(listed, all_scores[:, None, :], 0.0), axis=-1) * logit_scale
    student_log = jax.nn.log_softmax(student, axis=-1)
    teacher_log = jax.nn.log_softmax(teacher, axis=-1)
    teacher_prob = jnp.exp(teacher_log)
    losses = jnp.sum(teacher_prob * (teacher_log - student_log), axis=-1)
    logit_grad = logit_scale * (jnp.exp(student_log) - teacher_prob)
    row_grad = jnp.sum(jnp.where(listed, logit_grad[..., None], 0.0), axis=1)
    received_wide = received.astype(jnp.float32)
    owner_grads = lax.all_gather(row_grad, "section", axis=0, tiled=True)
    received_grad = jnp.dot(
        owner_grads.T, owner_queries.astype(jnp.float32), precision=lax.Precision.HIGHEST
    ).astype(jnp.bfloat16)
    query_grad = jnp.dot(row_grad, received_wide, precision=lax.Precision.HIGHEST)
    returned = lax.all_to_all(received_grad, "dp", split_axis=0, concat_axis=0, tiled=True)
    spots = jnp.arange(rows)
    back = jnp.sum(jnp.where(route[0][None, :] == spots[:, None], spots[None, :], 0), axis=1)
    pool_grad = rows_at(returned, back)
    return (held_out, losses, query_grad, pool_grad)


def solution(mesh):
    return jax.shard_map(
        on_device,
        mesh=mesh,
        in_specs=(
            P(None, "dp", None),
            P("section", "dp", None),
            P("section", None, "dp"),
            P("section", None),
            P(),
            P("dp", None),
            P("dp", None),
            P(("section", "dp"), None),
            P(("section", "dp"), None),
            P(("section", "dp"), None),
        ),
        out_specs=(
            P("section", "dp", None),
            P(("section", "dp")),
            P(("section", "dp"), None),
            P("dp", None),
        ),
        check_vma=False,
    )
```

profile of v0, /device:TPU:0, one launch (start us, length us, event | category | flops | bytes accessed | tf_op | source)
XLA Modules:
  0.0 312.5 jit_solution(17875827913129519498)
XLA Ops:
  1.2 4.9 %shard_map.129 = bf16[2048,512]{1,0:T(8,128)(2,1)} custom-call(s32[4]{0:T(128)} %add_subtract_fusion.at_ref, bf16[4096,512]{1,0:T(8,128)(2,1)} %bitcast.85, f32[8,1,512]{2,1,0:T(1,128)} %bitcast.94), custom_call_target="tpu_custom_call" | custom-call | flops 1048576 | bytes 4194304 | tf_op jit(solution)/shard_map/pallas_call | solution.py:33
  6.1 5.0 %collective-permute-start.10 = (bf16[2048,512]{1,0:T(8,128)(2,1)}, bf16[2048,512]{1,0:T(8,128)(2,1)S(1)}, u32[]{:S(2)}, u32[]{:S(2)}) collective-permute-start(bf16[2048,512]{1,0:T(8,128)(2,1)} %shard_map.129), channel_id=1, source_target_pairs={{0,1},{1,0},{2,3},{3,2},{4,5},{5,4},{6,7},{7,6}} | collective-permute-start | bytes 6291464 | tf_op jit(solution)/shard_map/ppermute | solution.py:173
  22.6 6.3 %all-to-all-start.1 = ((bf16[8,8,4736]{2,1,0:T(8,128)(2,1)}), bf16[8,8,4736]{2,1,0:T(8,128)(2,1)}, u32[]{:S(2)}, u32[]{:S(2)}) async-start(bf16[8,8,4736]{2,1,0:T(8,128)(2,1)} %pad_maximum_fusion.3), calls=%async_computation.1 | async-start | bytes 1212416 | tf_op jit(solution)/shard_map/all_to_all | solution.py:241
  32.1 4.9 %shard_map.131.weight_ref = bf16[2048,512]{1,0:T(8,128)(2,1)} custom-call(s32[4]{0:T(128)} %fusion.25.at_ref, bf16[4096,512]{1,0:T(8,128)(2,1)} %bitcast.86, f32[8,1,512]{2,1,0:T(1,128)} %bitcast.95), custom_call_target="tpu_custom_call" | custom-call | flops 1048576 | bytes 4194304 | tf_op jit(solution)/shard_map/pallas_call | solution.py:33
  38.0 33.9 %collective-permute-done = bf16[192,2048]{1,0:T(8,128)(2,1)} collective-permute-done((bf16[192,2048]{1,0:T(8,128)(2,1)}, bf16[192,2048]{1,0:T(8,128)(2,1)}, u32[]{:S(2)}, u32[]{:S(2)}) %collective-permute-start) | collective-permute-done | bytes 786464 | tf_op jit(solution)/shard_map/ppermute | solution.py:173
  84.1 4.5 %collective-permute-start.8 = (bf16[128,2048]{1,0:T(8,128)(2,1)S(1)}, bf16[128,2048]{1,0:T(8,128)(2,1)}, u32[]{:S(2)}, u32[]{:S(2)}) collective-permute-start(bf16[128,2048]{1,0:T(8,128)(2,1)S(1)} %maximum_select_fusion.2.refs_0_), channel_id=1, source_target_pairs={{0,4},{1,5},{2,6},{3,7},{4,0},{5,1},{6,2},{7,3}} | collective-permute-start | bytes 1572872 | tf_op jit(solution)/shard_map/ppermute | solution.py:173
  90.6 6.2 %all_gather.15 = bf16[32,4096]{1,0:T(8,128)(2,1)} all-gather(bf16[8,4096]{1,0:T(8,128)(2,1)S(1)} %copy-done.22), channel_id=1, replica_groups=mesh['section'=4,'dp'=8] {'section'}, dimensions={0}, use_global_device_ids=true | all-gather | bytes 327680 | tf_op jit(solution)/shard_map/all_gather | solution.py:242
  98.5 6.0 %all-to-all-start.2 = ((bf16[8,4,512]{2,1,0:T(4,128)(2,1)}), bf16[8,4,512]{2,1,0:T(4,128)(2,1)S(1)}, u32[]{:S(2)}, u32[]{:S(2)}) async-start(bf16[8,4,512]{2,1,0:T(4,128)(2,1)} %broadcast_in_dim.63), calls=%async_computation.2 | async-start | bytes 65536 | tf_op jit(solution)/shard_map/all_to_all | solution.py:286
  104.5 3.9 %collective-permute-start.4 = (bf16[128,2048]{1,0:T(8,128)(2,1)}, bf16[128,2048]{1,0:T(8,128)(2,1)}, u32[]{:S(2)}, u32[]{:S(2)}) collective-permute-start(bf16[128,2048]{1,0:T(8,128)(2,1)} %maximum_select_fusion.1.refs_0_), channel_id=1, source_target_pairs={{0,2},{1,3},{2,0},{3,1},{4,6},{5,7},{6,4},{7,5}} | collective-permute-start | bytes 1572872 | tf_op jit(solution)/shard_map/ppermute | solution.py:173
  108.5 4.3 %collective-permute-start.5 = (bf16[128,2048]{1,0:T(8,128)(2,1)}, bf16[128,2048]{1,0:T(8,128)(2,1)}, u32[]{:S(2)}, u32[]{:S(2)}) collective-permute-start(bf16[128,2048]{1,0:T(8,128)(2,1)} %maximum_select_fusion.1.refs_0_), channel_id=1, source_target_pairs={{0,4},{1,5},{2,6},{3,7},{4,0},{5,1},{6,2},{7,3}} | collective-permute-start | bytes 1572872 | tf_op jit(solution)/shard_map/ppermute | solution.py:173
  128.5 7.3 %collective-permute-done.11.other_ref = bf16[512,640]{1,0:T(8,128)(2,1)} collective-permute-done((bf16[512,640]{1,0:T(8,128)(2,1)}, bf16[512,640]{1,0:T(8,128)(2,1)}, u32[]{:S(2)}, u32[]{:S(2)}) %collective-permute-start.11) | collective-permute-done | bytes 655392 | tf_op jit(solution)/shard_map/ppermute | solution.py:173
  145.7 5.2 %collective-permute-start.1 = (bf16[128,2048]{1,0:T(8,128)(2,1)S(1)}, bf16[128,2048]{1,0:T(8,128)(2,1)}, u32[]{:S(2)}, u32[]{:S(2)}) collective-permute-start(bf16[128,2048]{1,0:T(8,128)(2,1)S(1)} %maximum_select_fusion.refs_0_), channel_id=1, source_target_pairs={{0,2},{1,3},{2,0},{3,1},{4,6},{5,7},{6,4},{7,5}} | collective-permute-start | bytes 1572872 | tf_op jit(solution)/shard_map/ppermute | solution.py:173
  160.8 4.0 %shard_map.133 = (bf16[512,640]{1,0:T(8,128)(2,1)}, f32[512,128]{1,0:T(8,128)S(1)}, bf16[512,2048]{1,0:T(8,128)(2,1)S(1)}) custom-call(s32[3]{0:T(128)S(1)} %pad_add_fusion.at_ref, bf16[128,2048]{1,0:T(8,128)(2,1)} %maximum_select_fusion.1.refs_0_, bf16[128,2048]{1,0:T(8,128)(2,1)} %collective-permute-done.4.refs_1_, ...), custom_call_target="tpu_custom_call" | custom-call | flops 1073741824 | bytes 4194304 | tf_op jit(solution)/shard_map/pallas_call | solution.py:121
  164.8 3.9 %collective-permute-start.17 = (bf16[512,640]{1,0:T(8,128)(2,1)}, bf16[512,640]{1,0:T(8,128)(2,1)}, u32[]{:S(2)}, u32[]{:S(2)}) collective-permute-start(bf16[512,640]{1,0:T(8,128)(2,1)} %get-tuple-element.18), channel_id=1, source_target_pairs={{0,1},{1,0},{2,3},{3,2},{4,5},{5,4},{6,7},{7,6},{8,9},{9,8},{10,11... | collective-permute-start | bytes 1966088 | tf_op jit(solution)/shard_map/ppermute | solution.py:173
  171.7 22.0 %all-to-all-start.3 = ((bf16[8,4,512]{2,1,0:T(4,128)(2,1)}), bf16[8,4,512]{2,1,0:T(4,128)(2,1)S(1)}, u32[]{:S(2)}, u32[]{:S(2)}) async-start(bf16[8,4,512]{2,1,0:T(4,128)(2,1)} %broadcast_in_dim.64), calls=%async_computation.3 | async-start | bytes 65536 | tf_op jit(solution)/shard_map/all_to_all | solution.py:286
  194.7 5.7 %all-to-all-done.3 = bf16[8,4,512]{2,1,0:T(4,128)(2,1)S(1)} async-done(((bf16[8,4,512]{2,1,0:T(4,128)(2,1)}), bf16[8,4,512]{2,1,0:T(4,128)(2,1)S(1)}, u32[]{:S(2)}, u32[]{:S(2)}) %all-to-all-start.3) | async-done | bytes 32800 | tf_op jit(solution)/shard_map/all_to_all | solution.py:286
  213.1 19.1 %all-gather.1 = bf16[4,12,512]{2,1,0:T(8,128)(2,1)S(1)} all-gather(bf16[1,12,512]{2,1,0:T(8,128)(2,1)S(1)} %maximum_bitcast_fusion), channel_id=2, replica_groups=mesh['section'=4,'dp'=8] {'section'}, dimensions={0}, use_global_device_ids=true | all-gather | bytes 61440 | tf_op jit(solution)/shard_map/all_gather | solution.py:309
  232.8 4.0 %all-to-all-start.4 = ((bf16[8,12,512]{2,1,0:T(8,128)(2,1)}), bf16[8,12,512]{2,1,0:T(8,128)(2,1)}, u32[]{:S(2)}, u32[]{:S(2)}) async-start(bf16[8,12,512]{2,1,0:T(8,128)(2,1)} %broadcast_in_dim.104), calls=%async_computation.4 | async-start | bytes 262144 | tf_op jit(solution)/shard_map/all_to_all | solution.py:286
  239.0 4.5 %shard_map.135 = (bf16[512,640]{1,0:T(8,128)(2,1)}, f32[512,128]{1,0:T(8,128)S(1)}, bf16[512,2048]{1,0:T(8,128)(2,1)S(1)}) custom-call(s32[3]{0:T(128)S(1)} %pad_add_fusion.at_ref, bf16[128,2048]{1,0:T(8,128)(2,1)S(1)} %maximum_select_fusion.refs_0_, bf16[128,2048]{1,0:T(8,128)(2,1)} %collective-permute-done.1.refs_1_, ...), custom_call_target="tpu_custom_call" | custom-call | flops 1073741824 | bytes 4194304 | tf_op jit(solution)/shard_map/pallas_call | solution.py:121
  253.3 5.2 %collective-permute-done.22.other_ref = bf16[512,640]{1,0:T(8,128)(2,1)S(1)} collective-permute-done((bf16[512,640]{1,0:T(8,128)(2,1)}, bf16[512,640]{1,0:T(8,128)(2,1)S(1)}, u32[]{:S(2)}, u32[]{:S(2)}) %collective-permute-start.22) | collective-permute-done | bytes 655392 | tf_op jit(solution)/shard_map/ppermute | solution.py:173
  261.3 8.2 %all-to-all-start = ((bf16[8,64,512]{2,1,0:T(8,128)(2,1)}), bf16[8,64,512]{2,1,0:T(8,128)(2,1)S(1)}, u32[]{:S(2)}, u32[]{:S(2)}) async-start(bf16[8,64,512]{2,1,0:T(8,128)(2,1)} %bitcast.9), calls=%async_computation | async-start | bytes 1048576 | tf_op jit(solution)/shard_map/all_to_all | solution.py:281
  272.1 14.4 %all_gather.14 = f32[32,64]{1,0:T(8,128)S(1)} all-gather(f32[8,64]{1,0:T(8,128)S(1)} %select_reduce_fusion), channel_id=1, replica_groups=mesh['section'=4,'dp'=8] {'section'}, dimensions={0}, use_global_device_ids=true | all-gather | bytes 10240 | tf_op jit(solution)/shard_map/all_gather | solution.py:340
  288.0 6.0 %all-to-all-start.5 = ((bf16[8,8,4096]{2,1,0:T(8,128)(2,1)}), bf16[8,8,4096]{2,1,0:T(8,128)(2,1)S(1)}, u32[]{:S(2)}, u32[]{:S(2)}) async-start(bf16[8,8,4096]{2,1,0:T(8,128)(2,1)} %fusion.1), calls=%async_computation.5 | async-start | bytes 1048576 | tf_op jit(solution)/shard_map/all_to_all | solution.py:345
  297.1 11.8 %all-to-all-done.5 = bf16[8,8,4096]{2,1,0:T(8,128)(2,1)S(1)} async-done(((bf16[8,8,4096]{2,1,0:T(8,128)(2,1)}), bf16[8,8,4096]{2,1,0:T(8,128)(2,1)S(1)}, u32[]{:S(2)}, u32[]{:S(2)}) %all-to-all-start.5) | async-done | bytes 524320 | tf_op jit(solution)/shard_map/all_to_all | solution.py:345
  (191 shorter events, 110.0 us)
Async XLA Ops:
  6.1 108.6 %collective-permute-start.10 = (bf16[2048,512]{1,0:T(8,128)(2,1)}, bf16[2048,512]{1,0:T(8,128)(2,1)S(1)}, u32[]{:S(2)}, u32[]{:S(2)}) collective-permute-start(bf16[2048,512]{1,0:T(8,128)(2,1)} %shard_map.129), channel_id=1, source_target_pairs={{0,1},{1,0},{2,3},{3,2},{4,5},{5,4},{6,7},{7,6}} | collective-permute-start | bytes 6291464 | tf_op jit(solution)/shard_map/ppermute | solution.py:173
  11.1 133.1 %collective-permute-start.16 = (bf16[2048,512]{1,0:T(8,128)(2,1)}, bf16[2048,512]{1,0:T(8,128)(2,1)}, u32[]{:S(2)}, u32[]{:S(2)}) collective-permute-start(bf16[2048,512]{1,0:T(8,128)(2,1)} %shard_map.129), channel_id=1, source_target_pairs={{8,9},{9,8},{10,11},{11,10},{12,13},{13,12},{14,15},{15,14},{16,17... | collective-permute-start | bytes 6291464 | tf_op jit(solution)/shard_map/ppermute | solution.py:173
  15.9 56.0 %collective-permute-start = (bf16[192,2048]{1,0:T(8,128)(2,1)}, bf16[192,2048]{1,0:T(8,128)(2,1)}, u32[]{:S(2)}, u32[]{:S(2)}) collective-permute-start(bf16[192,2048]{1,0:T(8,128)(2,1)} %get-tuple-element.26), channel_id=1, source_target_pairs={{0,1},{1,0},{2,3},{3,2},{4,5},{5,4},{6,7},{7,6}} | collective-permute-start | bytes 2359304 | tf_op jit(solution)/shard_map/ppermute | solution.py:173
  22.6 51.3 %all-to-all-start.1 = ((bf16[8,8,4736]{2,1,0:T(8,128)(2,1)}), bf16[8,8,4736]{2,1,0:T(8,128)(2,1)}, u32[]{:S(2)}, u32[]{:S(2)}) async-start(bf16[8,8,4736]{2,1,0:T(8,128)(2,1)} %pad_maximum_fusion.3), calls=%async_computation.1 | async-start | bytes 1212416 | tf_op jit(solution)/shard_map/all_to_all | solution.py:241
  80.4 24.1 %collective-permute-start.7 = (bf16[128,2048]{1,0:T(8,128)(2,1)S(1)}, bf16[128,2048]{1,0:T(8,128)(2,1)}, u32[]{:S(2)}, u32[]{:S(2)}) collective-permute-start(bf16[128,2048]{1,0:T(8,128)(2,1)S(1)} %maximum_select_fusion.2.refs_0_), channel_id=1, source_target_pairs={{0,2},{1,3},{2,0},{3,1},{4,6},{5,7},{6,4},{7,5}} | collective-permute-start | bytes 1572872 | tf_op jit(solution)/shard_map/ppermute | solution.py:173
  84.1 24.3 %collective-permute-start.8 = (bf16[128,2048]{1,0:T(8,128)(2,1)S(1)}, bf16[128,2048]{1,0:T(8,128)(2,1)}, u32[]{:S(2)}, u32[]{:S(2)}) collective-permute-start(bf16[128,2048]{1,0:T(8,128)(2,1)S(1)} %maximum_select_fusion.2.refs_0_), channel_id=1, source_target_pairs={{0,4},{1,5},{2,6},{3,7},{4,0},{5,1},{6,2},{7,3}} | collective-permute-start | bytes 1572872 | tf_op jit(solution)/shard_map/ppermute | solution.py:173
  88.7 24.1 %collective-permute-start.9 = (bf16[128,2048]{1,0:T(8,128)(2,1)S(1)}, bf16[128,2048]{1,0:T(8,128)(2,1)}, u32[]{:S(2)}, u32[]{:S(2)}) collective-permute-start(bf16[128,2048]{1,0:T(8,128)(2,1)S(1)} %maximum_select_fusion.2.refs_0_), channel_id=1, source_target_pairs={{0,6},{1,7},{2,4},{3,5},{4,2},{5,3},{6,0},{7,1}} | collective-permute-start | bytes 1572872 | tf_op jit(solution)/shard_map/ppermute | solution.py:173
  98.5 29.7 %all-to-all-start.2 = ((bf16[8,4,512]{2,1,0:T(4,128)(2,1)}), bf16[8,4,512]{2,1,0:T(4,128)(2,1)S(1)}, u32[]{:S(2)}, u32[]{:S(2)}) async-start(bf16[8,4,512]{2,1,0:T(4,128)(2,1)} %broadcast_in_dim.63), calls=%async_computation.2 | async-start | bytes 65536 | tf_op jit(solution)/shard_map/all_to_all | solution.py:286
  104.5 36.9 %collective-permute-start.4 = (bf16[128,2048]{1,0:T(8,128)(2,1)}, bf16[128,2048]{1,0:T(8,128)(2,1)}, u32[]{:S(2)}, u32[]{:S(2)}) collective-permute-start(bf16[128,2048]{1,0:T(8,128)(2,1)} %maximum_select_fusion.1.refs_0_), channel_id=1, source_target_pairs={{0,2},{1,3},{2,0},{3,1},{4,6},{5,7},{6,4},{7,5}} | collective-permute-start | bytes 1572872 | tf_op jit(solution)/shard_map/ppermute | solution.py:173
  108.5 34.3 %collective-permute-start.5 = (bf16[128,2048]{1,0:T(8,128)(2,1)}, bf16[128,2048]{1,0:T(8,128)(2,1)}, u32[]{:S(2)}, u32[]{:S(2)}) collective-permute-start(bf16[128,2048]{1,0:T(8,128)(2,1)} %maximum_select_fusion.1.refs_0_), channel_id=1, source_target_pairs={{0,4},{1,5},{2,6},{3,7},{4,0},{5,1},{6,2},{7,3}} | collective-permute-start | bytes 1572872 | tf_op jit(solution)/shard_map/ppermute | solution.py:173
  112.8 33.0 %collective-permute-start.6 = (bf16[128,2048]{1,0:T(8,128)(2,1)}, bf16[128,2048]{1,0:T(8,128)(2,1)}, u32[]{:S(2)}, u32[]{:S(2)}) collective-permute-start(bf16[128,2048]{1,0:T(8,128)(2,1)} %maximum_select_fusion.1.refs_0_), channel_id=1, source_target_pairs={{0,6},{1,7},{2,4},{3,5},{4,2},{5,3},{6,0},{7,1}} | collective-permute-start | bytes 1572872 | tf_op jit(solution)/shard_map/ppermute | solution.py:173
  144.1 16.6 %collective-permute-start.15 = (bf16[512,512]{1,0:T(8,128)(2,1)S(1)}, bf16[512,512]{1,0:T(8,128)(2,1)S(1)}, u32[]{:S(2)}, u32[]{:S(2)}) collective-permute-start(bf16[512,512]{1,0:T(8,128)(2,1)S(1)} %shard_map.132), channel_id=1, source_target_pairs={{0,14},{1,15},{2,12},{3,13},{4,10},{5,11},{6,8},{7,9}} | collective-permute-start | bytes 1572872 | tf_op jit(solution)/shard_map/ppermute | solution.py:173
  145.7 65.7 %collective-permute-start.1 = (bf16[128,2048]{1,0:T(8,128)(2,1)S(1)}, bf16[128,2048]{1,0:T(8,128)(2,1)}, u32[]{:S(2)}, u32[]{:S(2)}) collective-permute-start(bf16[128,2048]{1,0:T(8,128)(2,1)S(1)} %maximum_select_fusion.refs_0_), channel_id=1, source_target_pairs={{0,2},{1,3},{2,0},{3,1},{4,6},{5,7},{6,4},{7,5}} | collective-permute-start | bytes 1572872 | tf_op jit(solution)/shard_map/ppermute | solution.py:173
  150.9 86.4 %collective-permute-start.2 = (bf16[128,2048]{1,0:T(8,128)(2,1)S(1)}, bf16[128,2048]{1,0:T(8,128)(2,1)}, u32[]{:S(2)}, u32[]{:S(2)}) collective-permute-start(bf16[128,2048]{1,0:T(8,128)(2,1)S(1)} %maximum_select_fusion.refs_0_), channel_id=1, source_target_pairs={{0,4},{1,5},{2,6},{3,7},{4,0},{5,1},{6,2},{7,3}} | collective-permute-start | bytes 1572872 | tf_op jit(solution)/shard_map/ppermute | solution.py:173
  154.2 83.1 %collective-permute-start.3 = (bf16[128,2048]{1,0:T(8,128)(2,1)S(1)}, bf16[128,2048]{1,0:T(8,128)(2,1)}, u32[]{:S(2)}, u32[]{:S(2)}) collective-permute-start(bf16[128,2048]{1,0:T(8,128)(2,1)S(1)} %maximum_select_fusion.refs_0_), channel_id=1, source_target_pairs={{0,6},{1,7},{2,4},{3,5},{4,2},{5,3},{6,0},{7,1}} | collective-permute-start | bytes 1572872 | tf_op jit(solution)/shard_map/ppermute | solution.py:173
  164.8 35.7 %collective-permute-start.17 = (bf16[512,640]{1,0:T(8,128)(2,1)}, bf16[512,640]{1,0:T(8,128)(2,1)}, u32[]{:S(2)}, u32[]{:S(2)}) collective-permute-start(bf16[512,640]{1,0:T(8,128)(2,1)} %get-tuple-element.18), channel_id=1, source_target_pairs={{0,1},{1,0},{2,3},{3,2},{4,5},{5,4},{6,7},{7,6},{8,9},{9,8},{10,11... | collective-permute-start | bytes 1966088 | tf_op jit(solution)/shard_map/ppermute | solution.py:173
  171.7 28.6 %all-to-all-start.3 = ((bf16[8,4,512]{2,1,0:T(4,128)(2,1)}), bf16[8,4,512]{2,1,0:T(4,128)(2,1)S(1)}, u32[]{:S(2)}, u32[]{:S(2)}) async-start(bf16[8,4,512]{2,1,0:T(4,128)(2,1)} %broadcast_in_dim.64), calls=%async_computation.3 | async-start | bytes 65536 | tf_op jit(solution)/shard_map/all_to_all | solution.py:286
  208.5 28.8 %collective-permute-start.19 = (bf16[512,512]{1,0:T(8,128)(2,1)}, bf16[512,512]{1,0:T(8,128)(2,1)}, u32[]{:S(2)}, u32[]{:S(2)}) collective-permute-start(bf16[512,512]{1,0:T(8,128)(2,1)} %collective-permute-done.18.refs_4_), channel_id=1, source_target_pairs={{8,10},{9,11},{10,8},{11,9},{12,14},{13,15},{14,12},{15,13},{16,18... | collective-permute-start | bytes 1572872 | tf_op jit(solution)/shard_map/ppermute | solution.py:173
  210.0 27.4 %collective-permute-start.20 = (bf16[512,512]{1,0:T(8,128)(2,1)}, bf16[512,512]{1,0:T(8,128)(2,1)}, u32[]{:S(2)}, u32[]{:S(2)}) collective-permute-start(bf16[512,512]{1,0:T(8,128)(2,1)} %collective-permute-done.18.refs_4_), channel_id=1, source_target_pairs={{8,12},{9,13},{10,14},{11,15},{12,8},{13,9},{14,10},{15,11},{16,20... | collective-permute-start | bytes 1572872 | tf_op jit(solution)/shard_map/ppermute | solution.py:173
  211.4 25.9 %collective-permute-start.21 = (bf16[512,512]{1,0:T(8,128)(2,1)}, bf16[512,512]{1,0:T(8,128)(2,1)}, u32[]{:S(2)}, u32[]{:S(2)}) collective-permute-start(bf16[512,512]{1,0:T(8,128)(2,1)} %collective-permute-done.18.refs_4_), channel_id=1, source_target_pairs={{8,14},{9,15},{10,12},{11,13},{12,10},{13,11},{14,8},{15,9},{16,22... | collective-permute-start | bytes 1572872 | tf_op jit(solution)/shard_map/ppermute | solution.py:173
  232.8 15.8 %all-to-all-start.4 = ((bf16[8,12,512]{2,1,0:T(8,128)(2,1)}), bf16[8,12,512]{2,1,0:T(8,128)(2,1)}, u32[]{:S(2)}, u32[]{:S(2)}) async-start(bf16[8,12,512]{2,1,0:T(8,128)(2,1)} %broadcast_in_dim.104), calls=%async_computation.4 | async-start | bytes 262144 | tf_op jit(solution)/shard_map/all_to_all | solution.py:286
  261.3 26.6 %all-to-all-start = ((bf16[8,64,512]{2,1,0:T(8,128)(2,1)}), bf16[8,64,512]{2,1,0:T(8,128)(2,1)S(1)}, u32[]{:S(2)}, u32[]{:S(2)}) async-start(bf16[8,64,512]{2,1,0:T(8,128)(2,1)} %bitcast.9), calls=%async_computation | async-start | bytes 1048576 | tf_op jit(solution)/shard_map/all_to_all | solution.py:281
  288.0 21.0 %all-to-all-start.5 = ((bf16[8,8,4096]{2,1,0:T(8,128)(2,1)}), bf16[8,8,4096]{2,1,0:T(8,128)(2,1)S(1)}, u32[]{:S(2)}, u32[]{:S(2)}) async-start(bf16[8,8,4096]{2,1,0:T(8,128)(2,1)} %fusion.1), calls=%async_computation.5 | async-start | bytes 1048576 | tf_op jit(solution)/shard_map/all_to_all | solution.py:345
  294.1 16.5 %collective-permute-start.23 = (bf16[64,4096]{1,0:T(8,128)(2,1)S(1)}, bf16[64,4096]{1,0:T(8,128)(2,1)S(1)}, u32[]{:S(2)}, u32[]{:S(2)}) collective-permute-start(bf16[64,4096]{1,0:T(8,128)(2,1)S(1)} %bitcast.93), channel_id=1, source_target_pairs={{0,8},{1,9},{2,10},{3,11},{4,12},{5,13},{6,14},{7,15},{8,16},{9,17... | collective-permute-start | bytes 1572872 | tf_op jit(solution)/shard_map/ppermute | solution.py:173
  (38 other events, 396.5 us)
where the time goes:
time: 315 us; the launch traced here: 313 us
  starting transfers between devices  121 us (38%)
  waiting for transfers between devices  67.5 us (21%)
  blocking collectives  39.7 us (13%)
  Pallas kernels  30.5 us (10%)
  local copies, waits for them, and re-layouts  23.6 us (7%)
  other arithmetic  18.9 us (6%)
  matrix products  10.1 us (3%)
    ppermute x26, starting transfers between devices, send(): lax.ppermute(x, AXES, [(a * dps + i, b * dps + (i ^ flip)) for a, b, flip...  68.4 us
    ppermute x26, waiting for transfers between devices, send(): lax.ppermute(x, AXES, [(a * dps + i, b * dps + (i ^ flip)) for a, b, flip...  50 us
    all_to_all x3, starting transfers between devices, spread(): lax.all_to_all(jnp.broadcast_to(x[None], (dps, *x.shape)), 'dp', split_ax...  32 us
    all_gather x1, blocking collectives, on_device(): lax.all_gather(jnp.concatenate(exits, axis=0), 'section', axis=0)  19.1 us
    all_gather x1, blocking collectives, on_device(): owner_grads = lax.all_gather(row_grad, 'section', axis=0, tiled=True)  14.4 us
    pallas_call x3, Pallas kernels, sent_half(): pl.pallas_call(functools.partial(sent_kernel, len(row_piles)), out_shape=...  12.4 us
    all_to_all x1, waiting for transfers between devices, on_device(): lax.all_to_all(received_grad, 'dp', split_axis=0, concat_axis=0, tiled=True)  11.8 us
    unnamed x65, local copies, waits for them, and re-layouts  11.3 us
  transfers between devices with their start and end apart: 32, of which 7 were waited for; matrix products, arithmetic and copies ran while one was open for 13% of the time, Pallas kernels for 7%

commit v1 on v0

--- a/solution.py
+++ b/solution.py
@@ -200,30 +200,21 @@
             jnp.arange(half), list(range(last_full + 1))
         )
 
-    used = list(range(last_full + 1))
-
-    def sides(x):
-        pieces = [x[:, k * cols : (k + 1) * cols] for k in range(dps)]
-        even, odd = jnp.concatenate(pieces[0::2], axis=1), jnp.concatenate(pieces[1::2], axis=1)
-        return jnp.where(side == 0, even, odd), jnp.where(side == 0, odd, even)
-
-    entries = jnp.concatenate([held_states[0], *fresh_batches[: TICKS - 1]], axis=0)
-    stay, leave = sides(entries)
-    came = send(leave, [(a, a, 1) for a in used])
-
-    def gathered(i, owners):
-        here, there = stay[i * tok : (i + 1) * tok], came[i * tok : (i + 1) * tok]
-        pair = jnp.where(
-            side == 0,
-            jnp.concatenate([here, there], axis=0),
-            jnp.concatenate([there, here], axis=0),
-        )
-        return [pair] + [send(pair, [(a, a, 2 * k) for a in owners]) for k in range(1, half)]
-
-    entry_piles = gathered(0, used)
-    fresh_piles = []
-    for i in range(TICKS - 1):
-        fresh_piles.append(gathered(i + 1, [0]))
+    helpers = [sections - TICKS + 1 + i for i in range(TICKS - 1)]
+    used = list(range(last_full + 1)) + helpers
+    entry = held_states[0]
+    for helper, fresh in zip(helpers, fresh_batches):
+        entry = jnp.where(section == helper, fresh, entry)
+    pieces = [entry[:, k * cols : (k + 1) * cols] for k in range(dps)]
+    even, odd = jnp.concatenate(pieces[0::2], axis=1), jnp.concatenate(pieces[1::2], axis=1)
+    here, leave = jnp.where(side == 0, even, odd), jnp.where(side == 0, odd, even)
+    there = send(leave, [(a, a, 1) for a in used])
+    pair = jnp.where(
+        side == 0,
+        jnp.concatenate([here, there], axis=0),
+        jnp.concatenate([there, here], axis=0),
+    )
+    entry_piles = [pair] + [send(pair, [(a, a, 2 * k) for a in used]) for k in range(1, half)]
 
     rows = cached_pool.shape[0]
     per_peer = rows // dps
@@ -245,9 +236,9 @@
         at = jnp.stack([jnp.asarray(x, jnp.int32) for x in at])
         part, square, states = sent_half(at, row_piles, column_piles, theirs)
         other = send(part, hops)
-        return kept_half(at, states, mine, other, square, width, pair_rows)
-
-    block = layer(
+        return kept_half(at, states, mine, other, square, width, pair_rows), states
+
+    block, states = layer(
         entry_piles,
         [],
         mine_first,
@@ -255,6 +246,9 @@
         (1, place, place),
         [(a, a, 1) for a in range(last_full + 1)],
     )
+    fresh_states = []
+    for helper in helpers:
+        fresh_states.append(send(states, [(helper, 0, 0)]))
     first = section == 0
     row_order = jnp.where(first, place, 0)
     for tick in range(1, TICKS):
@@ -270,8 +264,8 @@
                 send(block, [(a, a, 2 * k) for a in range(1, top + 1)])
                 for k in range(1, half)
             ]
-        block = layer(
-            fresh_piles[tick - 1],
+        block, _ = layer(
+            [fresh_states[tick - 1]],
             piles,
             mine_late,
             theirs_late,

time: 315 us -> 304 us (0.965)
  starting transfers between devices: 121 us -> 85.3 us
  waiting for transfers between devices: 67.5 us -> 91.7 us
  other arithmetic: 18.9 us -> 25.5 us
  local copies, waits for them, and re-layouts: 23.6 us -> 17.7 us
    ppermute x26 -> x22, waiting for transfers between devices: 50 us -> 74.6 us  [send(): lax.ppermute(x, AXES, [(a * dps + i, b * dps + (i ^ flip)) for a, b, flip...]
    ppermute x26 -> x22, starting transfers between devices: 68.4 us -> 48.8 us  [send(): lax.ppermute(x, AXES, [(a * dps + i, b * dps + (i ^ flip)) for a, b, flip...]
    all_to_all x3, starting transfers between devices: 32 us -> 15 us  [spread(): lax.all_to_all(jnp.broadcast_to(x[None], (dps, *x.shape)), 'dp', split_ax...]
    all_gather x1, blocking collectives: 6.23 us -> 11.6 us  [on_device(): owner_queries = lax.all_gather(queries, 'section', axis=0, tiled=True)]
    unnamed x65 -> x59, local copies, waits for them, and re-layouts: 11.3 us -> 7.65 us
    all_gather x1, blocking collectives: 19.1 us -> 15.9 us  [on_device(): lax.all_gather(jnp.concatenate(exits, axis=0), 'section', axis=0)]
  transfers between devices with their start and end apart: 32 -> 28, of which waited for: 7 -> 9; matrix products, arithmetic and copies ran while one was open for 13% -> 13% of each run, Pallas kernels for 7% -> 9%
where the time goes in v1:
time: 304 us; the launch traced here: 301 us
  waiting for transfers between devices  91.7 us (30%)
  starting transfers between devices  85.3 us (28%)
  blocking collectives  40.5 us (13%)
  Pallas kernels  30.6 us (10%)
  other arithmetic  25.5 us (8%)
  local copies, waits for them, and re-layouts  17.7 us (6%)
  matrix products  8.81 us (3%)
    ppermute x22, waiting for transfers between devices, send(): lax.ppermute(x, AXES, [(a * dps + i, b * dps + (i ^ flip)) for a, b, flip...  74.6 us
    ppermute x22, starting transfers between devices, send(): lax.ppermute(x, AXES, [(a * dps + i, b * dps + (i ^ flip)) for a, b, flip...  48.8 us
    all_gather x1, blocking collectives, on_device(): lax.all_gather(jnp.concatenate(exits, axis=0), 'section', axis=0)  15.9 us
    all_to_all x3, starting transfers between devices, spread(): lax.all_to_all(jnp.broadcast_to(x[None], (dps, *x.shape)), 'dp', split_ax...  15 us
    all_gather x1, blocking collectives, on_device(): owner_grads = lax.all_gather(row_grad, 'section', axis=0, tiled=True)  13.1 us
    pallas_call x3, Pallas kernels, sent_half(): pl.pallas_call(functools.partial(sent_kernel, len(row_piles)), out_shape=...  12.7 us
    all_to_all x1, waiting for transfers between devices, on_device(): lax.all_to_all(received_grad, 'dp', split_axis=0, concat_axis=0, tiled=True)  11.8 us
    all_gather x1, blocking collectives, on_device(): owner_queries = lax.all_gather(queries, 'section', axis=0, tiled=True)  11.6 us
  transfers between devices with their start and end apart: 28, of which 9 were waited for; matrix products, arithmetic and copies ran while one was open for 13% of the time, Pallas kernels for 9%

profile of v1, /device:TPU:0, one launch (start us, length us, event | category | flops | bytes accessed | tf_op | source)
XLA Modules:
  0.0 301.5 jit_solution(3189800127140436083)
XLA Ops:
  4.9 7.3 %all-to-all-start.1 = ((bf16[8,8,4736]{2,1,0:T(8,128)(2,1)}), bf16[8,8,4736]{2,1,0:T(8,128)(2,1)}, u32[]{:S(2)}, u32[]{:S(2)}) async-start(bf16[8,8,4736]{2,1,0:T(8,128)(2,1)} %pad_maximum_fusion), calls=%async_computation.1 | async-start | bytes 1212416 | tf_op jit(solution)/shard_map/all_to_all | solution.py:232
  12.7 5.0 %shard_map.129 = bf16[2048,512]{1,0:T(8,128)(2,1)} custom-call(s32[4]{0:T(128)} %add_subtract_fusion.at_ref, bf16[4096,512]{1,0:T(8,128)(2,1)} %bitcast.82, f32[8,1,512]{2,1,0:T(1,128)} %bitcast.90), custom_call_target="tpu_custom_call" | custom-call | flops 1048576 | bytes 4194304 | tf_op jit(solution)/shard_map/pallas_call | solution.py:33
  17.7 3.9 %collective-permute-start.4 = (bf16[2048,512]{1,0:T(8,128)(2,1)}, bf16[2048,512]{1,0:T(8,128)(2,1)S(1)}, u32[]{:S(2)}, u32[]{:S(2)}) collective-permute-start(bf16[2048,512]{1,0:T(8,128)(2,1)} %shard_map.129), channel_id=1, source_target_pairs={{0,1},{1,0},{2,3},{3,2},{4,5},{5,4},{6,7},{7,6}} | collective-permute-start | bytes 6291464 | tf_op jit(solution)/shard_map/ppermute | solution.py:173
  31.8 40.5 %collective-permute-done = bf16[64,2048]{1,0:T(8,128)(2,1)S(1)} collective-permute-done((bf16[64,2048]{1,0:T(8,128)(2,1)S(1)}, bf16[64,2048]{1,0:T(8,128)(2,1)S(1)}, u32[]{:S(2)}, u32[]{:S(2)}) %collective-permute-start) | collective-permute-done | bytes 262176 | tf_op jit(solution)/shard_map/ppermute | solution.py:173
  74.2 4.6 %collective-permute-start.3 = (bf16[128,2048]{1,0:T(8,128)(2,1)S(1)}, bf16[128,2048]{1,0:T(8,128)(2,1)}, u32[]{:S(2)}, u32[]{:S(2)}) collective-permute-start(bf16[128,2048]{1,0:T(8,128)(2,1)S(1)} %maximum_select_fusion.refs_0_), channel_id=1, source_target_pairs={{0,6},{1,7},{2,4},{3,5},{4,2},{5,3},{6,0},{7,1},{16,22},{17,23},{1... | collective-permute-start | bytes 1572872 | tf_op jit(solution)/shard_map/ppermute | solution.py:173
  87.3 16.1 %collective-permute-done.2.refs_2_ = bf16[128,2048]{1,0:T(8,128)(2,1)} collective-permute-done((bf16[128,2048]{1,0:T(8,128)(2,1)S(1)}, bf16[128,2048]{1,0:T(8,128)(2,1)}, u32[]{:S(2)}, u32[]{:S(2)}) %collective-permute-start.2) | collective-permute-done | bytes 524320 | tf_op jit(solution)/shard_map/ppermute | solution.py:173
  112.9 4.9 %shard_map.131.weight_ref = bf16[2048,512]{1,0:T(8,128)(2,1)} custom-call(s32[4]{0:T(128)} %fusion.25.at_ref, bf16[4096,512]{1,0:T(8,128)(2,1)} %bitcast.83, f32[8,1,512]{2,1,0:T(1,128)} %bitcast.91), custom_call_target="tpu_custom_call" | custom-call | flops 1048576 | bytes 4194304 | tf_op jit(solution)/shard_map/pallas_call | solution.py:33
  118.4 4.2 %all-to-all-start.2 = ((bf16[8,4,512]{2,1,0:T(4,128)(2,1)}), bf16[8,4,512]{2,1,0:T(4,128)(2,1)}, u32[]{:S(2)}, u32[]{:S(2)}) async-start(bf16[8,4,512]{2,1,0:T(4,128)(2,1)} %broadcast_in_dim.63), calls=%async_computation.2 | async-start | bytes 65536 | tf_op jit(solution)/shard_map/all_to_all | solution.py:280
  122.6 3.9 %collective-permute-start.7 = (bf16[512,640]{1,0:T(8,128)(2,1)}, bf16[512,640]{1,0:T(8,128)(2,1)S(1)}, u32[]{:S(2)}, u32[]{:S(2)}) collective-permute-start(bf16[512,640]{1,0:T(8,128)(2,1)} %copy-done.9), channel_id=1, source_target_pairs={{0,1},{1,0},{2,3},{3,2},{4,5},{5,4},{6,7},{7,6}} | collective-permute-start | bytes 1966088 | tf_op jit(solution)/shard_map/ppermute | solution.py:173
  126.5 11.6 %all_gather.15 = bf16[32,4096]{1,0:T(8,128)(2,1)} all-gather(bf16[8,4096]{1,0:T(8,128)(2,1)} %param.18), channel_id=1, replica_groups=mesh['section'=4,'dp'=8] {'section'}, dimensions={0}, use_global_device_ids=true | all-gather | bytes 327680 | tf_op jit(solution)/shard_map/all_gather | solution.py:233
  145.4 4.8 %collective-permute-start.11 = (bf16[512,512]{1,0:T(8,128)(2,1)S(1)}, bf16[512,512]{1,0:T(8,128)(2,1)S(1)}, u32[]{:S(2)}, u32[]{:S(2)}) collective-permute-start(bf16[512,512]{1,0:T(8,128)(2,1)S(1)} %shard_map.132), channel_id=1, source_target_pairs={{0,14},{1,15},{2,12},{3,13},{4,10},{5,11},{6,8},{7,9}} | collective-permute-start | bytes 1572872 | tf_op jit(solution)/shard_map/ppermute | solution.py:173
  158.2 4.3 %collective-permute-done.10.refs_3_ = bf16[512,512]{1,0:T(8,128)(2,1)S(1)} collective-permute-done((bf16[512,512]{1,0:T(8,128)(2,1)S(1)}, bf16[512,512]{1,0:T(8,128)(2,1)S(1)}, u32[]{:S(2)}, u32[]{:S(2)}) %collective-permute-start.10) | collective-permute-done | bytes 524320 | tf_op jit(solution)/shard_map/ppermute | solution.py:173
  162.5 5.6 %collective-permute-done.9.refs_2_ = bf16[512,512]{1,0:T(8,128)(2,1)S(1)} collective-permute-done((bf16[512,512]{1,0:T(8,128)(2,1)S(1)}, bf16[512,512]{1,0:T(8,128)(2,1)S(1)}, u32[]{:S(2)}, u32[]{:S(2)}) %collective-permute-start.9) | collective-permute-done | bytes 524320 | tf_op jit(solution)/shard_map/ppermute | solution.py:173
  168.1 4.1 %shard_map.133 = (bf16[512,640]{1,0:T(8,128)(2,1)}, f32[512,128]{1,0:T(8,128)S(1)}, bf16[512,2048]{1,0:T(8,128)(2,1)S(1)}) custom-call(s32[3]{0:T(128)S(1)} %pad_add_fusion.at_ref, bf16[512,2048]{1,0:T(8,128)(2,1)} %collective-permute-done.6.refs_0_, bf16[512,512]{1,0:T(8,128)(2,1)S(1)} %collective-permute-done.8.refs_1_, ...), custom_call_target="tpu_custom_call" | custom-call | flops 1073741824 | bytes 4194304 | tf_op jit(solution)/shard_map/pallas_call | solution.py:121
  179.0 6.8 %all-to-all-start.3 = ((bf16[8,4,512]{2,1,0:T(4,128)(2,1)}), bf16[8,4,512]{2,1,0:T(4,128)(2,1)}, u32[]{:S(2)}, u32[]{:S(2)}) async-start(bf16[8,4,512]{2,1,0:T(4,128)(2,1)} %broadcast_in_dim.64), calls=%async_computation.3 | async-start | bytes 65536 | tf_op jit(solution)/shard_map/all_to_all | solution.py:280
  187.3 5.3 %all-to-all-done.3 = bf16[8,4,512]{2,1,0:T(4,128)(2,1)} async-done(((bf16[8,4,512]{2,1,0:T(4,128)(2,1)}), bf16[8,4,512]{2,1,0:T(4,128)(2,1)}, u32[]{:S(2)}, u32[]{:S(2)}) %all-to-all-start.3) | async-done | bytes 32800 | tf_op jit(solution)/shard_map/all_to_all | solution.py:280
  206.1 15.9 %all-gather.1 = bf16[4,12,512]{2,1,0:T(8,128)(2,1)S(1)} all-gather(bf16[1,12,512]{2,1,0:T(8,128)(2,1)S(1)} %maximum_bitcast_fusion), channel_id=2, replica_groups=mesh['section'=4,'dp'=8] {'section'}, dimensions={0}, use_global_device_ids=true | all-gather | bytes 61440 | tf_op jit(solution)/shard_map/all_gather | solution.py:303
  222.6 4.0 %all-to-all-start.4 = ((bf16[8,12,512]{2,1,0:T(8,128)(2,1)}), bf16[8,12,512]{2,1,0:T(8,128)(2,1)}, u32[]{:S(2)}, u32[]{:S(2)}) async-start(bf16[8,12,512]{2,1,0:T(8,128)(2,1)} %broadcast_in_dim.104), calls=%async_computation.4 | async-start | bytes 262144 | tf_op jit(solution)/shard_map/all_to_all | solution.py:280
  228.3 4.7 %shard_map.135 = (bf16[512,640]{1,0:T(8,128)(2,1)}, f32[512,128]{1,0:T(8,128)S(1)}, bf16[512,2048]{1,0:T(8,128)(2,1)S(1)}) custom-call(s32[3]{0:T(128)S(1)} %pad_add_fusion.at_ref, bf16[512,2048]{1,0:T(8,128)(2,1)} %collective-permute-done.5.refs_0_, bf16[512,512]{1,0:T(8,128)(2,1)S(1)} %collective-permute-done.14.refs_1_, ...), custom_call_target="tpu_custom_call" | custom-call | flops 1073741824 | bytes 4194304 | tf_op jit(solution)/shard_map/pallas_call | solution.py:121
  242.8 4.4 %collective-permute-done.18.other_ref = bf16[512,640]{1,0:T(8,128)(2,1)S(1)} collective-permute-done((bf16[512,640]{1,0:T(8,128)(2,1)}, bf16[512,640]{1,0:T(8,128)(2,1)S(1)}, u32[]{:S(2)}, u32[]{:S(2)}) %collective-permute-start.18) | collective-permute-done | bytes 655392 | tf_op jit(solution)/shard_map/ppermute | solution.py:173
  250.1 8.3 %all-to-all-start = ((bf16[8,64,512]{2,1,0:T(8,128)(2,1)}), bf16[8,64,512]{2,1,0:T(8,128)(2,1)S(1)}, u32[]{:S(2)}, u32[]{:S(2)}) async-start(bf16[8,64,512]{2,1,0:T(8,128)(2,1)} %bitcast.7), calls=%async_computation | async-start | bytes 1048576 | tf_op jit(solution)/shard_map/all_to_all | solution.py:275
  261.6 13.1 %all_gather.14 = f32[32,64]{1,0:T(8,128)S(1)} all-gather(f32[8,64]{1,0:T(8,128)S(1)} %select_reduce_fusion), channel_id=1, replica_groups=mesh['section'=4,'dp'=8] {'section'}, dimensions={0}, use_global_device_ids=true | all-gather | bytes 10240 | tf_op jit(solution)/shard_map/all_gather | solution.py:334
  277.0 5.9 %all-to-all-start.5 = ((bf16[8,8,4096]{2,1,0:T(8,128)(2,1)}), bf16[8,8,4096]{2,1,0:T(8,128)(2,1)S(1)}, u32[]{:S(2)}, u32[]{:S(2)}) async-start(bf16[8,8,4096]{2,1,0:T(8,128)(2,1)} %fusion.1), calls=%async_computation.5 | async-start | bytes 1048576 | tf_op jit(solution)/shard_map/all_to_all | solution.py:339
  286.1 11.8 %all-to-all-done.5 = bf16[8,8,4096]{2,1,0:T(8,128)(2,1)S(1)} async-done(((bf16[8,8,4096]{2,1,0:T(8,128)(2,1)}), bf16[8,8,4096]{2,1,0:T(8,128)(2,1)S(1)}, u32[]{:S(2)}, u32[]{:S(2)}) %all-to-all-start.5) | async-done | bytes 524320 | tf_op jit(solution)/shard_map/all_to_all | solution.py:339
  (172 shorter events, 99.2 us)
Async XLA Ops:
  4.9 80.4 %all-to-all-start.1 = ((bf16[8,8,4736]{2,1,0:T(8,128)(2,1)}), bf16[8,8,4736]{2,1,0:T(8,128)(2,1)}, u32[]{:S(2)}, u32[]{:S(2)}) async-start(bf16[8,8,4736]{2,1,0:T(8,128)(2,1)} %pad_maximum_fusion), calls=%async_computation.1 | async-start | bytes 1212416 | tf_op jit(solution)/shard_map/all_to_all | solution.py:232
  17.7 85.7 %collective-permute-start.4 = (bf16[2048,512]{1,0:T(8,128)(2,1)}, bf16[2048,512]{1,0:T(8,128)(2,1)S(1)}, u32[]{:S(2)}, u32[]{:S(2)}) collective-permute-start(bf16[2048,512]{1,0:T(8,128)(2,1)} %shard_map.129), channel_id=1, source_target_pairs={{0,1},{1,0},{2,3},{3,2},{4,5},{5,4},{6,7},{7,6}} | collective-permute-start | bytes 6291464 | tf_op jit(solution)/shard_map/ppermute | solution.py:173
  24.6 47.7 %collective-permute-start = (bf16[64,2048]{1,0:T(8,128)(2,1)S(1)}, bf16[64,2048]{1,0:T(8,128)(2,1)S(1)}, u32[]{:S(2)}, u32[]{:S(2)}) collective-permute-start(bf16[64,2048]{1,0:T(8,128)(2,1)S(1)} %get-tuple-element.26), channel_id=1, source_target_pairs={{0,1},{1,0},{2,3},{3,2},{4,5},{5,4},{6,7},{7,6},{16,17},{17,16},{1... | collective-permute-start | bytes 786440 | tf_op jit(solution)/shard_map/ppermute | solution.py:173
  26.6 126.3 %collective-permute-start.12 = (bf16[2048,512]{1,0:T(8,128)(2,1)}, bf16[2048,512]{1,0:T(8,128)(2,1)}, u32[]{:S(2)}, u32[]{:S(2)}) collective-permute-start(bf16[2048,512]{1,0:T(8,128)(2,1)} %shard_map.129), channel_id=1, source_target_pairs={{8,9},{9,8},{10,11},{11,10},{12,13},{13,12},{14,15},{15,14},{16,17... | collective-permute-start | bytes 6291464 | tf_op jit(solution)/shard_map/ppermute | solution.py:173
  74.2 13.1 %collective-permute-start.3 = (bf16[128,2048]{1,0:T(8,128)(2,1)S(1)}, bf16[128,2048]{1,0:T(8,128)(2,1)}, u32[]{:S(2)}, u32[]{:S(2)}) collective-permute-start(bf16[128,2048]{1,0:T(8,128)(2,1)S(1)} %maximum_select_fusion.refs_0_), channel_id=1, source_target_pairs={{0,6},{1,7},{2,4},{3,5},{4,2},{5,3},{6,0},{7,1},{16,22},{17,23},{1... | collective-permute-start | bytes 1572872 | tf_op jit(solution)/shard_map/ppermute | solution.py:173
  78.7 24.6 %collective-permute-start.2 = (bf16[128,2048]{1,0:T(8,128)(2,1)S(1)}, bf16[128,2048]{1,0:T(8,128)(2,1)}, u32[]{:S(2)}, u32[]{:S(2)}) collective-permute-start(bf16[128,2048]{1,0:T(8,128)(2,1)S(1)} %maximum_select_fusion.refs_0_), channel_id=1, source_target_pairs={{0,4},{1,5},{2,6},{3,7},{4,0},{5,1},{6,2},{7,3},{16,20},{17,21},{1... | collective-permute-start | bytes 1572872 | tf_op jit(solution)/shard_map/ppermute | solution.py:173
  81.2 22.2 %collective-permute-start.1 = (bf16[128,2048]{1,0:T(8,128)(2,1)S(1)}, bf16[128,2048]{1,0:T(8,128)(2,1)}, u32[]{:S(2)}, u32[]{:S(2)}) collective-permute-start(bf16[128,2048]{1,0:T(8,128)(2,1)S(1)} %maximum_select_fusion.refs_0_), channel_id=1, source_target_pairs={{0,2},{1,3},{2,0},{3,1},{4,6},{5,7},{6,4},{7,5},{16,18},{17,19},{1... | collective-permute-start | bytes 1572872 | tf_op jit(solution)/shard_map/ppermute | solution.py:173
  107.3 60.8 %collective-permute-start.6 = (bf16[512,2048]{1,0:T(8,128)(2,1)}, bf16[512,2048]{1,0:T(8,128)(2,1)}, u32[]{:S(2)}, u32[]{:S(2)}) collective-permute-start(bf16[512,2048]{1,0:T(8,128)(2,1)} %get-tuple-element.14.states_ref), channel_id=1, source_target_pairs={{16,0},{17,1},{18,2},{19,3},{20,4},{21,5},{22,6},{23,7}} | collective-permute-start | bytes 6291464 | tf_op jit(solution)/shard_map/ppermute | solution.py:173
  118.4 19.7 %all-to-all-start.2 = ((bf16[8,4,512]{2,1,0:T(4,128)(2,1)}), bf16[8,4,512]{2,1,0:T(4,128)(2,1)}, u32[]{:S(2)}, u32[]{:S(2)}) async-start(bf16[8,4,512]{2,1,0:T(4,128)(2,1)} %broadcast_in_dim.63), calls=%async_computation.2 | async-start | bytes 65536 | tf_op jit(solution)/shard_map/all_to_all | solution.py:280
  122.6 18.1 %collective-permute-start.7 = (bf16[512,640]{1,0:T(8,128)(2,1)}, bf16[512,640]{1,0:T(8,128)(2,1)S(1)}, u32[]{:S(2)}, u32[]{:S(2)}) collective-permute-start(bf16[512,640]{1,0:T(8,128)(2,1)} %copy-done.9), channel_id=1, source_target_pairs={{0,1},{1,0},{2,3},{3,2},{4,5},{5,4},{6,7},{7,6}} | collective-permute-start | bytes 1966088 | tf_op jit(solution)/shard_map/ppermute | solution.py:173
  150.2 12.4 %collective-permute-start.10 = (bf16[512,512]{1,0:T(8,128)(2,1)S(1)}, bf16[512,512]{1,0:T(8,128)(2,1)S(1)}, u32[]{:S(2)}, u32[]{:S(2)}) collective-permute-start(bf16[512,512]{1,0:T(8,128)(2,1)S(1)} %shard_map.132), channel_id=1, source_target_pairs={{0,12},{1,13},{2,14},{3,15},{4,8},{5,9},{6,10},{7,11}} | collective-permute-start | bytes 1572872 | tf_op jit(solution)/shard_map/ppermute | solution.py:173
  151.5 16.6 %collective-permute-start.9 = (bf16[512,512]{1,0:T(8,128)(2,1)S(1)}, bf16[512,512]{1,0:T(8,128)(2,1)S(1)}, u32[]{:S(2)}, u32[]{:S(2)}) collective-permute-start(bf16[512,512]{1,0:T(8,128)(2,1)S(1)} %shard_map.132), channel_id=1, source_target_pairs={{0,10},{1,11},{2,8},{3,9},{4,14},{5,15},{6,12},{7,13}} | collective-permute-start | bytes 1572872 | tf_op jit(solution)/shard_map/ppermute | solution.py:173
  152.8 15.3 %collective-permute-start.8 = (bf16[512,512]{1,0:T(8,128)(2,1)S(1)}, bf16[512,512]{1,0:T(8,128)(2,1)S(1)}, u32[]{:S(2)}, u32[]{:S(2)}) collective-permute-start(bf16[512,512]{1,0:T(8,128)(2,1)S(1)} %shard_map.132), channel_id=1, source_target_pairs={{0,8},{1,9},{2,10},{3,11},{4,12},{5,13},{6,14},{7,15}} | collective-permute-start | bytes 1572872 | tf_op jit(solution)/shard_map/ppermute | solution.py:173
  156.9 69.8 %collective-permute-start.5 = (bf16[512,2048]{1,0:T(8,128)(2,1)}, bf16[512,2048]{1,0:T(8,128)(2,1)}, u32[]{:S(2)}, u32[]{:S(2)}) collective-permute-start(bf16[512,2048]{1,0:T(8,128)(2,1)} %get-tuple-element.14.states_ref), channel_id=1, source_target_pairs={{24,0},{25,1},{26,2},{27,3},{28,4},{29,5},{30,6},{31,7}} | collective-permute-start | bytes 6291464 | tf_op jit(solution)/shard_map/ppermute | solution.py:173
  172.3 22.0 %collective-permute-start.13 = (bf16[512,640]{1,0:T(8,128)(2,1)}, bf16[512,640]{1,0:T(8,128)(2,1)S(1)}, u32[]{:S(2)}, u32[]{:S(2)}) collective-permute-start(bf16[512,640]{1,0:T(8,128)(2,1)} %get-tuple-element.18), channel_id=1, source_target_pairs={{0,1},{1,0},{2,3},{3,2},{4,5},{5,4},{6,7},{7,6},{8,9},{9,8},{10,11... | collective-permute-start | bytes 1966088 | tf_op jit(solution)/shard_map/ppermute | solution.py:173
  179.0 13.6 %all-to-all-start.3 = ((bf16[8,4,512]{2,1,0:T(4,128)(2,1)}), bf16[8,4,512]{2,1,0:T(4,128)(2,1)}, u32[]{:S(2)}, u32[]{:S(2)}) async-start(bf16[8,4,512]{2,1,0:T(4,128)(2,1)} %broadcast_in_dim.64), calls=%async_computation.3 | async-start | bytes 65536 | tf_op jit(solution)/shard_map/all_to_all | solution.py:280
  201.7 25.0 %collective-permute-start.17 = (bf16[512,512]{1,0:T(8,128)(2,1)S(1)}, bf16[512,512]{1,0:T(8,128)(2,1)}, u32[]{:S(2)}, u32[]{:S(2)}) collective-permute-start(bf16[512,512]{1,0:T(8,128)(2,1)S(1)} %collective-permute-done.14.refs_1_), channel_id=1, source_target_pairs={{8,14},{9,15},{10,12},{11,13},{12,10},{13,11},{14,8},{15,9},{16,22... | collective-permute-start | bytes 1572872 | tf_op jit(solution)/shard_map/ppermute | solution.py:173
  203.2 23.5 %collective-permute-start.16 = (bf16[512,512]{1,0:T(8,128)(2,1)S(1)}, bf16[512,512]{1,0:T(8,128)(2,1)}, u32[]{:S(2)}, u32[]{:S(2)}) collective-permute-start(bf16[512,512]{1,0:T(8,128)(2,1)S(1)} %collective-permute-done.14.refs_1_), channel_id=1, source_target_pairs={{8,12},{9,13},{10,14},{11,15},{12,8},{13,9},{14,10},{15,11},{16,20... | collective-permute-start | bytes 1572872 | tf_op jit(solution)/shard_map/ppermute | solution.py:173
  204.6 22.1 %collective-permute-start.15 = (bf16[512,512]{1,0:T(8,128)(2,1)S(1)}, bf16[512,512]{1,0:T(8,128)(2,1)}, u32[]{:S(2)}, u32[]{:S(2)}) collective-permute-start(bf16[512,512]{1,0:T(8,128)(2,1)S(1)} %collective-permute-done.14.refs_1_), channel_id=1, source_target_pairs={{8,10},{9,11},{10,8},{11,9},{12,14},{13,15},{14,12},{15,13},{16,18... | collective-permute-start | bytes 1572872 | tf_op jit(solution)/shard_map/ppermute | solution.py:173
  222.6 15.5 %all-to-all-start.4 = ((bf16[8,12,512]{2,1,0:T(8,128)(2,1)}), bf16[8,12,512]{2,1,0:T(8,128)(2,1)}, u32[]{:S(2)}, u32[]{:S(2)}) async-start(bf16[8,12,512]{2,1,0:T(8,128)(2,1)} %broadcast_in_dim.104), calls=%async_computation.4 | async-start | bytes 262144 | tf_op jit(solution)/shard_map/all_to_all | solution.py:280
  234.3 12.9 %collective-permute-start.18 = (bf16[512,640]{1,0:T(8,128)(2,1)}, bf16[512,640]{1,0:T(8,128)(2,1)S(1)}, u32[]{:S(2)}, u32[]{:S(2)}) collective-permute-start(bf16[512,640]{1,0:T(8,128)(2,1)} %get-tuple-element.21), channel_id=1, source_target_pairs={{0,1},{1,0},{2,3},{3,2},{4,5},{5,4},{6,7},{7,6},{8,9},{9,8},{10,11... | collective-permute-start | bytes 1966088 | tf_op jit(solution)/shard_map/ppermute | solution.py:173
  250.1 26.9 %all-to-all-start = ((bf16[8,64,512]{2,1,0:T(8,128)(2,1)}), bf16[8,64,512]{2,1,0:T(8,128)(2,1)S(1)}, u32[]{:S(2)}, u32[]{:S(2)}) async-start(bf16[8,64,512]{2,1,0:T(8,128)(2,1)} %bitcast.7), calls=%async_computation | async-start | bytes 1048576 | tf_op jit(solution)/shard_map/all_to_all | solution.py:275
  277.0 20.9 %all-to-all-start.5 = ((bf16[8,8,4096]{2,1,0:T(8,128)(2,1)}), bf16[8,8,4096]{2,1,0:T(8,128)(2,1)S(1)}, u32[]{:S(2)}, u32[]{:S(2)}) async-start(bf16[8,8,4096]{2,1,0:T(8,128)(2,1)} %fusion.1), calls=%async_computation.5 | async-start | bytes 1048576 | tf_op jit(solution)/shard_map/all_to_all | solution.py:339
  283.1 16.5 %collective-permute-start.19 = (bf16[64,4096]{1,0:T(8,128)(2,1)S(1)}, bf16[64,4096]{1,0:T(8,128)(2,1)S(1)}, u32[]{:S(2)}, u32[]{:S(2)}) collective-permute-start(bf16[64,4096]{1,0:T(8,128)(2,1)S(1)} %bitcast.89), channel_id=1, source_target_pairs={{0,8},{1,9},{2,10},{3,11},{4,12},{5,13},{6,14},{7,15},{8,16},{9,17... | collective-permute-start | bytes 1572872 | tf_op jit(solution)/shard_map/ppermute | solution.py:173
  (31 other events, 412.5 us)

commit v2 on v0

--- a/solution.py
+++ b/solution.py
@@ -200,19 +200,17 @@
             jnp.arange(half), list(range(last_full + 1))
         )
 
-    used = list(range(last_full + 1))
+    helper = sections - TICKS + 1
+    used = list(range(last_full + 1)) + [helper]
 
     def sides(x):
         pieces = [x[:, k * cols : (k + 1) * cols] for k in range(dps)]
         even, odd = jnp.concatenate(pieces[0::2], axis=1), jnp.concatenate(pieces[1::2], axis=1)
         return jnp.where(side == 0, even, odd), jnp.where(side == 0, odd, even)
 
-    entries = jnp.concatenate([held_states[0], *fresh_batches[: TICKS - 1]], axis=0)
-    stay, leave = sides(entries)
-    came = send(leave, [(a, a, 1) for a in used])
-
-    def gathered(i, owners):
-        here, there = stay[i * tok : (i + 1) * tok], came[i * tok : (i + 1) * tok]
+    def gathered(x, owners):
+        here, leave = sides(x)
+        there = send(leave, [(a, a, 1) for a in owners])
         pair = jnp.where(
             side == 0,
             jnp.concatenate([here, there], axis=0),
@@ -220,10 +218,9 @@
         )
         return [pair] + [send(pair, [(a, a, 2 * k) for a in owners]) for k in range(1, half)]
 
-    entry_piles = gathered(0, used)
-    fresh_piles = []
-    for i in range(TICKS - 1):
-        fresh_piles.append(gathered(i + 1, [0]))
+    entry = jnp.where(section == helper, fresh_batches[0], held_states[0])
+    entry_piles = gathered(entry, used)
+    fresh_piles = [gathered(fresh_batches[i], [0]) for i in range(1, TICKS - 1)]
 
     rows = cached_pool.shape[0]
     per_peer = rows // dps
@@ -245,9 +242,9 @@
         at = jnp.stack([jnp.asarray(x, jnp.int32) for x in at])
         part, square, states = sent_half(at, row_piles, column_piles, theirs)
         other = send(part, hops)
-        return kept_half(at, states, mine, other, square, width, pair_rows)
-
-    block = layer(
+        return kept_half(at, states, mine, other, square, width, pair_rows), states
+
+    block, states = layer(
         entry_piles,
         [],
         mine_first,
@@ -255,6 +252,7 @@
         (1, place, place),
         [(a, a, 1) for a in range(last_full + 1)],
     )
+    fresh_piles.insert(0, [send(states, [(helper, 0, 0)])])
     first = section == 0
     row_order = jnp.where(first, place, 0)
     for tick in range(1, TICKS):
@@ -270,7 +268,7 @@
                 send(block, [(a, a, 2 * k) for a in range(1, top + 1)])
                 for k in range(1, half)
             ]
-        block = layer(
+        block, _ = layer(
             fresh_piles[tick - 1],
             piles,
             mine_late,

time: 315 us -> 341 us (1.083)
  blocking collectives: 39.7 us -> 61.3 us
  waiting for transfers between devices: 67.5 us -> 75.8 us
  local copies, waits for them, and re-layouts: 23.6 us -> 17.4 us
    all_gather x1, blocking collectives: 6.23 us -> 27.3 us  [on_device(): owner_queries = lax.all_gather(queries, 'section', axis=0, tiled=True)]
    ppermute x26 -> x25, waiting for transfers between devices: 50 us -> 56.8 us  [send(): lax.ppermute(x, AXES, [(a * dps + i, b * dps + (i ^ flip)) for a, b, flip...]
    unnamed x65 -> x49, local copies, waits for them, and re-layouts: 11.3 us -> 8.49 us
    ppermute x26 -> x25, starting transfers between devices: 68.4 us -> 69.5 us  [send(): lax.ppermute(x, AXES, [(a * dps + i, b * dps + (i ^ flip)) for a, b, flip...]
  transfers between devices with their start and end apart: 32 -> 31, of which waited for: 7 -> 9; matrix products, arithmetic and copies ran while one was open for 13% -> 11% of each run, Pallas kernels for 7% -> 7%
where the time goes in v2:
time: 341 us; the launch traced here: 339 us
  starting transfers between devices  122 us (36%)
  waiting for transfers between devices  75.8 us (22%)
  blocking collectives  61.3 us (18%)
  Pallas kernels  31.2 us (9%)
  other arithmetic  21.6 us (6%)
  local copies, waits for them, and re-layouts  17.4 us (5%)
  matrix products  8.79 us (3%)
    ppermute x25, starting transfers between devices, send(): lax.ppermute(x, AXES, [(a * dps + i, b * dps + (i ^ flip)) for a, b, flip...  69.5 us
    ppermute x25, waiting for transfers between devices, send(): lax.ppermute(x, AXES, [(a * dps + i, b * dps + (i ^ flip)) for a, b, flip...  56.8 us
    all_to_all x3, starting transfers between devices, spread(): lax.all_to_all(jnp.broadcast_to(x[None], (dps, *x.shape)), 'dp', split_ax...  34.2 us
    all_gather x1, blocking collectives, on_device(): owner_queries = lax.all_gather(queries, 'section', axis=0, tiled=True)  27.3 us
    all_gather x1, blocking collectives, on_device(): lax.all_gather(jnp.concatenate(exits, axis=0), 'section', axis=0)  19.3 us
    all_gather x1, blocking collectives, on_device(): owner_grads = lax.all_gather(row_grad, 'section', axis=0, tiled=True)  14.7 us
    pallas_call x3, Pallas kernels, sent_half(): pl.pallas_call(functools.partial(sent_kernel, len(row_piles)), out_shape=...  12.5 us
    all_to_all x1, waiting for transfers between devices, on_device(): lax.all_to_all(received_grad, 'dp', split_axis=0, concat_axis=0, tiled=True)  11.8 us
  transfers between devices with their start and end apart: 31, of which 9 were waited for; matrix products, arithmetic and copies ran while one was open for 11% of the time, Pallas kernels for 7%

profile of v2, /device:TPU:0, one launch (start us, length us, event | category | flops | bytes accessed | tf_op | source)
XLA Modules:
  0.0 339.1 jit_solution(9276298148253023953)
XLA Ops:
  1.2 5.0 %shard_map.129 = bf16[2048,512]{1,0:T(8,128)(2,1)} custom-call(s32[4]{0:T(128)} %add_subtract_fusion.at_ref, bf16[4096,512]{1,0:T(8,128)(2,1)} %bitcast.84, f32[8,1,512]{2,1,0:T(1,128)} %bitcast.92), custom_call_target="tpu_custom_call" | custom-call | flops 1048576 | bytes 4194304 | tf_op jit(solution)/shard_map/pallas_call | solution.py:33
  6.2 4.9 %collective-permute-start.8 = (bf16[2048,512]{1,0:T(8,128)(2,1)}, bf16[2048,512]{1,0:T(8,128)(2,1)S(1)}, u32[]{:S(2)}, u32[]{:S(2)}) collective-permute-start(bf16[2048,512]{1,0:T(8,128)(2,1)} %shard_map.129), channel_id=1, source_target_pairs={{0,1},{1,0},{2,3},{3,2},{4,5},{5,4},{6,7},{7,6}} | collective-permute-start | bytes 6291464 | tf_op jit(solution)/shard_map/ppermute | solution.py:173
  16.0 4.9 %all-to-all-start.1 = ((bf16[8,8,4736]{2,1,0:T(8,128)(2,1)}), bf16[8,8,4736]{2,1,0:T(8,128)(2,1)}, u32[]{:S(2)}, u32[]{:S(2)}) async-start(bf16[8,8,4736]{2,1,0:T(8,128)(2,1)} %pad_maximum_fusion), calls=%async_computation.1 | async-start | bytes 1212416 | tf_op jit(solution)/shard_map/all_to_all | solution.py:238
  33.3 33.7 %collective-permute-done.4 = bf16[64,2048]{1,0:T(8,128)(2,1)S(1)} collective-permute-done((bf16[64,2048]{1,0:T(8,128)(2,1)S(1)}, bf16[64,2048]{1,0:T(8,128)(2,1)S(1)}, u32[]{:S(2)}, u32[]{:S(2)}) %collective-permute-start.4) | collective-permute-done | bytes 262176 | tf_op jit(solution)/shard_map/ppermute | solution.py:173
  72.6 4.5 %collective-permute-start.6 = (bf16[128,2048]{1,0:T(8,128)(2,1)S(1)}, bf16[128,2048]{1,0:T(8,128)(2,1)}, u32[]{:S(2)}, u32[]{:S(2)}) collective-permute-start(bf16[128,2048]{1,0:T(8,128)(2,1)S(1)} %maximum_select_fusion.1.refs_0_), channel_id=1, source_target_pairs={{0,4},{1,5},{2,6},{3,7},{4,0},{5,1},{6,2},{7,3},{16,20},{17,21},{1... | collective-permute-start | bytes 1572872 | tf_op jit(solution)/shard_map/ppermute | solution.py:173
  87.3 8.7 %collective-permute-done.6.refs_2_ = bf16[128,2048]{1,0:T(8,128)(2,1)} collective-permute-done((bf16[128,2048]{1,0:T(8,128)(2,1)S(1)}, bf16[128,2048]{1,0:T(8,128)(2,1)}, u32[]{:S(2)}, u32[]{:S(2)}) %collective-permute-start.6) | collective-permute-done | bytes 524320 | tf_op jit(solution)/shard_map/ppermute | solution.py:173
  104.2 27.3 %all_gather.15 = bf16[32,4096]{1,0:T(8,128)(2,1)} all-gather(bf16[8,4096]{1,0:T(8,128)(2,1)S(1)} %copy-done.14), channel_id=1, replica_groups=mesh['section'=4,'dp'=8] {'section'}, dimensions={0}, use_global_device_ids=true | all-gather | bytes 327680 | tf_op jit(solution)/shard_map/all_gather | solution.py:239
  132.7 4.9 %shard_map.131.weight_ref = bf16[2048,512]{1,0:T(8,128)(2,1)} custom-call(s32[4]{0:T(128)} %fusion.25.at_ref, bf16[4096,512]{1,0:T(8,128)(2,1)} %bitcast.85, f32[8,1,512]{2,1,0:T(1,128)} %bitcast.93), custom_call_target="tpu_custom_call" | custom-call | flops 1048576 | bytes 4194304 | tf_op jit(solution)/shard_map/pallas_call | solution.py:33
  138.2 9.4 %all-to-all-start.2 = ((bf16[8,4,512]{2,1,0:T(4,128)(2,1)}), bf16[8,4,512]{2,1,0:T(4,128)(2,1)S(1)}, u32[]{:S(2)}, u32[]{:S(2)}) async-start(bf16[8,4,512]{2,1,0:T(4,128)(2,1)} %broadcast_in_dim.63), calls=%async_computation.2 | async-start | bytes 65536 | tf_op jit(solution)/shard_map/all_to_all | solution.py:284
  154.6 5.8 %collective-permute-done.10.other_ref = bf16[512,640]{1,0:T(8,128)(2,1)} collective-permute-done((bf16[512,640]{1,0:T(8,128)(2,1)}, bf16[512,640]{1,0:T(8,128)(2,1)}, u32[]{:S(2)}, u32[]{:S(2)}) %collective-permute-start.10) | collective-permute-done | bytes 655392 | tf_op jit(solution)/shard_map/ppermute | solution.py:173
  170.9 4.1 %collective-permute-start.1 = (bf16[128,2048]{1,0:T(8,128)(2,1)S(1)}, bf16[128,2048]{1,0:T(8,128)(2,1)}, u32[]{:S(2)}, u32[]{:S(2)}) collective-permute-start(bf16[128,2048]{1,0:T(8,128)(2,1)S(1)} %maximum_select_fusion.refs_0_), channel_id=1, source_target_pairs={{0,2},{1,3},{2,0},{3,1},{4,6},{5,7},{6,4},{7,5}} | collective-permute-start | bytes 1572872 | tf_op jit(solution)/shard_map/ppermute | solution.py:173
  175.0 8.2 %collective-permute-start.2 = (bf16[128,2048]{1,0:T(8,128)(2,1)S(1)}, bf16[128,2048]{1,0:T(8,128)(2,1)}, u32[]{:S(2)}, u32[]{:S(2)}) collective-permute-start(bf16[128,2048]{1,0:T(8,128)(2,1)S(1)} %maximum_select_fusion.refs_0_), channel_id=1, source_target_pairs={{0,4},{1,5},{2,6},{3,7},{4,0},{5,1},{6,2},{7,3}} | collective-permute-start | bytes 1572872 | tf_op jit(solution)/shard_map/ppermute | solution.py:173
  183.2 4.8 %collective-permute-start.3 = (bf16[128,2048]{1,0:T(8,128)(2,1)S(1)}, bf16[128,2048]{1,0:T(8,128)(2,1)}, u32[]{:S(2)}, u32[]{:S(2)}) collective-permute-start(bf16[128,2048]{1,0:T(8,128)(2,1)S(1)} %maximum_select_fusion.refs_0_), channel_id=1, source_target_pairs={{0,6},{1,7},{2,4},{3,5},{4,2},{5,3},{6,0},{7,1}} | collective-permute-start | bytes 1572872 | tf_op jit(solution)/shard_map/ppermute | solution.py:173
  188.0 4.1 %shard_map.133 = (bf16[512,640]{1,0:T(8,128)(2,1)}, f32[512,128]{1,0:T(8,128)S(1)}, bf16[512,2048]{1,0:T(8,128)(2,1)S(1)}) custom-call(s32[3]{0:T(128)S(1)} %pad_add_fusion.at_ref, bf16[512,2048]{1,0:T(8,128)(2,1)} %collective-permute-done.9.refs_0_, bf16[512,512]{1,0:T(8,128)(2,1)S(1)} %collective-permute-done.11.refs_1_, ...), custom_call_target="tpu_custom_call" | custom-call | flops 1073741824 | bytes 4194304 | tf_op jit(solution)/shard_map/pallas_call | solution.py:121
  198.5 20.2 %all-to-all-start.3 = ((bf16[8,4,512]{2,1,0:T(4,128)(2,1)}), bf16[8,4,512]{2,1,0:T(4,128)(2,1)S(1)}, u32[]{:S(2)}, u32[]{:S(2)}) async-start(bf16[8,4,512]{2,1,0:T(4,128)(2,1)} %broadcast_in_dim.64), calls=%async_computation.3 | async-start | bytes 65536 | tf_op jit(solution)/shard_map/all_to_all | solution.py:284
  219.8 5.7 %all-to-all-done.3 = bf16[8,4,512]{2,1,0:T(4,128)(2,1)S(1)} async-done(((bf16[8,4,512]{2,1,0:T(4,128)(2,1)}), bf16[8,4,512]{2,1,0:T(4,128)(2,1)S(1)}, u32[]{:S(2)}, u32[]{:S(2)}) %all-to-all-start.3) | async-done | bytes 32800 | tf_op jit(solution)/shard_map/all_to_all | solution.py:284
  237.3 19.3 %all-gather.1 = bf16[4,12,512]{2,1,0:T(8,128)(2,1)S(1)} all-gather(bf16[1,12,512]{2,1,0:T(8,128)(2,1)S(1)} %maximum_bitcast_fusion), channel_id=2, replica_groups=mesh['section'=4,'dp'=8] {'section'}, dimensions={0}, use_global_device_ids=true | all-gather | bytes 61440 | tf_op jit(solution)/shard_map/all_gather | solution.py:307
  257.2 4.5 %all-to-all-start.4 = ((bf16[8,12,512]{2,1,0:T(8,128)(2,1)}), bf16[8,12,512]{2,1,0:T(8,128)(2,1)}, u32[]{:S(2)}, u32[]{:S(2)}) async-start(bf16[8,12,512]{2,1,0:T(8,128)(2,1)} %broadcast_in_dim.104), calls=%async_computation.4 | async-start | bytes 262144 | tf_op jit(solution)/shard_map/all_to_all | solution.py:284
  263.9 4.5 %shard_map.135 = (bf16[512,640]{1,0:T(8,128)(2,1)}, f32[512,128]{1,0:T(8,128)S(1)}, bf16[512,2048]{1,0:T(8,128)(2,1)S(1)}) custom-call(s32[3]{0:T(128)S(1)} %pad_add_fusion.at_ref, bf16[128,2048]{1,0:T(8,128)(2,1)S(1)} %maximum_select_fusion.refs_0_, bf16[128,2048]{1,0:T(8,128)(2,1)} %collective-permute-done.1.refs_1_, ...), custom_call_target="tpu_custom_call" | custom-call | flops 1073741824 | bytes 4194304 | tf_op jit(solution)/shard_map/pallas_call | solution.py:121
  278.4 5.9 %collective-permute-done.21.other_ref = bf16[512,640]{1,0:T(8,128)(2,1)S(1)} collective-permute-done((bf16[512,640]{1,0:T(8,128)(2,1)}, bf16[512,640]{1,0:T(8,128)(2,1)S(1)}, u32[]{:S(2)}, u32[]{:S(2)}) %collective-permute-start.21) | collective-permute-done | bytes 655392 | tf_op jit(solution)/shard_map/ppermute | solution.py:173
  287.1 7.2 %all-to-all-start = ((bf16[8,64,512]{2,1,0:T(8,128)(2,1)}), bf16[8,64,512]{2,1,0:T(8,128)(2,1)S(1)}, u32[]{:S(2)}, u32[]{:S(2)}) async-start(bf16[8,64,512]{2,1,0:T(8,128)(2,1)} %bitcast.8), calls=%async_computation | async-start | bytes 1048576 | tf_op jit(solution)/shard_map/all_to_all | solution.py:279
  297.5 14.7 %all_gather.14 = f32[32,64]{1,0:T(8,128)S(1)} all-gather(f32[8,64]{1,0:T(8,128)S(1)} %select_reduce_fusion), channel_id=1, replica_groups=mesh['section'=4,'dp'=8] {'section'}, dimensions={0}, use_global_device_ids=true | all-gather | bytes 10240 | tf_op jit(solution)/shard_map/all_gather | solution.py:338
  314.5 6.0 %all-to-all-start.5 = ((bf16[8,8,4096]{2,1,0:T(8,128)(2,1)}), bf16[8,8,4096]{2,1,0:T(8,128)(2,1)S(1)}, u32[]{:S(2)}, u32[]{:S(2)}) async-start(bf16[8,8,4096]{2,1,0:T(8,128)(2,1)} %fusion.1), calls=%async_computation.5 | async-start | bytes 1048576 | tf_op jit(solution)/shard_map/all_to_all | solution.py:343
  323.7 11.8 %all-to-all-done.5 = bf16[8,8,4096]{2,1,0:T(8,128)(2,1)S(1)} async-done(((bf16[8,8,4096]{2,1,0:T(8,128)(2,1)}), bf16[8,8,4096]{2,1,0:T(8,128)(2,1)S(1)}, u32[]{:S(2)}, u32[]{:S(2)}) %all-to-all-start.5) | async-done | bytes 524320 | tf_op jit(solution)/shard_map/all_to_all | solution.py:343
  (170 shorter events, 107.7 us)
Async XLA Ops:
  6.2 89.8 %collective-permute-start.8 = (bf16[2048,512]{1,0:T(8,128)(2,1)}, bf16[2048,512]{1,0:T(8,128)(2,1)S(1)}, u32[]{:S(2)}, u32[]{:S(2)}) collective-permute-start(bf16[2048,512]{1,0:T(8,128)(2,1)} %shard_map.129), channel_id=1, source_target_pairs={{0,1},{1,0},{2,3},{3,2},{4,5},{5,4},{6,7},{7,6}} | collective-permute-start | bytes 6291464 | tf_op jit(solution)/shard_map/ppermute | solution.py:173
  11.1 158.2 %collective-permute-start.15 = (bf16[2048,512]{1,0:T(8,128)(2,1)}, bf16[2048,512]{1,0:T(8,128)(2,1)}, u32[]{:S(2)}, u32[]{:S(2)}) collective-permute-start(bf16[2048,512]{1,0:T(8,128)(2,1)} %shard_map.129), channel_id=1, source_target_pairs={{8,9},{9,8},{10,11},{11,10},{12,13},{13,12},{14,15},{15,14},{16,17... | collective-permute-start | bytes 6291464 | tf_op jit(solution)/shard_map/ppermute | solution.py:173
  16.0 63.0 %all-to-all-start.1 = ((bf16[8,8,4736]{2,1,0:T(8,128)(2,1)}), bf16[8,8,4736]{2,1,0:T(8,128)(2,1)}, u32[]{:S(2)}, u32[]{:S(2)}) async-start(bf16[8,8,4736]{2,1,0:T(8,128)(2,1)} %pad_maximum_fusion), calls=%async_computation.1 | async-start | bytes 1212416 | tf_op jit(solution)/shard_map/all_to_all | solution.py:238
  25.1 41.9 %collective-permute-start.4 = (bf16[64,2048]{1,0:T(8,128)(2,1)S(1)}, bf16[64,2048]{1,0:T(8,128)(2,1)S(1)}, u32[]{:S(2)}, u32[]{:S(2)}) collective-permute-start(bf16[64,2048]{1,0:T(8,128)(2,1)S(1)} %get-tuple-element.28), channel_id=1, source_target_pairs={{0,1},{1,0},{2,3},{3,2},{4,5},{5,4},{6,7},{7,6},{16,17},{17,16},{1... | collective-permute-start | bytes 786440 | tf_op jit(solution)/shard_map/ppermute | solution.py:173
  72.6 23.4 %collective-permute-start.6 = (bf16[128,2048]{1,0:T(8,128)(2,1)S(1)}, bf16[128,2048]{1,0:T(8,128)(2,1)}, u32[]{:S(2)}, u32[]{:S(2)}) collective-permute-start(bf16[128,2048]{1,0:T(8,128)(2,1)S(1)} %maximum_select_fusion.1.refs_0_), channel_id=1, source_target_pairs={{0,4},{1,5},{2,6},{3,7},{4,0},{5,1},{6,2},{7,3},{16,20},{17,21},{1... | collective-permute-start | bytes 1572872 | tf_op jit(solution)/shard_map/ppermute | solution.py:173
  77.1 18.9 %collective-permute-start.7 = (bf16[128,2048]{1,0:T(8,128)(2,1)S(1)}, bf16[128,2048]{1,0:T(8,128)(2,1)}, u32[]{:S(2)}, u32[]{:S(2)}) collective-permute-start(bf16[128,2048]{1,0:T(8,128)(2,1)S(1)} %maximum_select_fusion.1.refs_0_), channel_id=1, source_target_pairs={{0,6},{1,7},{2,4},{3,5},{4,2},{5,3},{6,0},{7,1},{16,22},{17,23},{1... | collective-permute-start | bytes 1572872 | tf_op jit(solution)/shard_map/ppermute | solution.py:173
  83.4 68.1 %collective-permute-start = (bf16[64,2048]{1,0:T(8,128)(2,1)}, bf16[64,2048]{1,0:T(8,128)(2,1)}, u32[]{:S(2)}, u32[]{:S(2)}) collective-permute-start(bf16[64,2048]{1,0:T(8,128)(2,1)} %get-tuple-element.38), channel_id=1, source_target_pairs={{0,1},{1,0},{2,3},{3,2},{4,5},{5,4},{6,7},{7,6}} | collective-permute-start | bytes 786440 | tf_op jit(solution)/shard_map/ppermute | solution.py:173
  100.7 87.3 %collective-permute-start.9 = (bf16[512,2048]{1,0:T(8,128)(2,1)}, bf16[512,2048]{1,0:T(8,128)(2,1)}, u32[]{:S(2)}, u32[]{:S(2)}) collective-permute-start(bf16[512,2048]{1,0:T(8,128)(2,1)} %get-tuple-element.14.states_ref), channel_id=1, source_target_pairs={{16,0},{17,1},{18,2},{19,3},{20,4},{21,5},{22,6},{23,7}} | collective-permute-start | bytes 6291464 | tf_op jit(solution)/shard_map/ppermute | solution.py:173
  103.5 34.0 %collective-permute-start.23 = (bf16[4,512]{1,0:T(4,128)(2,1)S(1)}, bf16[4,512]{1,0:T(4,128)(2,1)S(1)}, u32[]{:S(2)}, u32[]{:S(2)}) collective-permute-start(bf16[4,512]{1,0:T(4,128)(2,1)S(1)} %fusion.20), channel_id=1, source_target_pairs={{8,16},{9,17},{10,18},{11,19},{12,20},{13,21},{14,22},{15,23},{16,... | collective-permute-start | bytes 12296 | tf_op jit(solution)/shard_map/ppermute | solution.py:173
  138.2 16.2 %all-to-all-start.2 = ((bf16[8,4,512]{2,1,0:T(4,128)(2,1)}), bf16[8,4,512]{2,1,0:T(4,128)(2,1)S(1)}, u32[]{:S(2)}, u32[]{:S(2)}) async-start(bf16[8,4,512]{2,1,0:T(4,128)(2,1)} %broadcast_in_dim.63), calls=%async_computation.2 | async-start | bytes 65536 | tf_op jit(solution)/shard_map/all_to_all | solution.py:284
  167.9 15.3 %collective-permute-start.13 = (bf16[512,512]{1,0:T(8,128)(2,1)S(1)}, bf16[512,512]{1,0:T(8,128)(2,1)S(1)}, u32[]{:S(2)}, u32[]{:S(2)}) collective-permute-start(bf16[512,512]{1,0:T(8,128)(2,1)S(1)} %shard_map.132), channel_id=1, source_target_pairs={{0,12},{1,13},{2,14},{3,15},{4,8},{5,9},{6,10},{7,11}} | collective-permute-start | bytes 1572872 | tf_op jit(solution)/shard_map/ppermute | solution.py:173
  169.3 18.7 %collective-permute-start.14 = (bf16[512,512]{1,0:T(8,128)(2,1)S(1)}, bf16[512,512]{1,0:T(8,128)(2,1)S(1)}, u32[]{:S(2)}, u32[]{:S(2)}) collective-permute-start(bf16[512,512]{1,0:T(8,128)(2,1)S(1)} %shard_map.132), channel_id=1, source_target_pairs={{0,14},{1,15},{2,12},{3,13},{4,10},{5,11},{6,8},{7,9}} | collective-permute-start | bytes 1572872 | tf_op jit(solution)/shard_map/ppermute | solution.py:173
  170.9 64.9 %collective-permute-start.1 = (bf16[128,2048]{1,0:T(8,128)(2,1)S(1)}, bf16[128,2048]{1,0:T(8,128)(2,1)}, u32[]{:S(2)}, u32[]{:S(2)}) collective-permute-start(bf16[128,2048]{1,0:T(8,128)(2,1)S(1)} %maximum_select_fusion.refs_0_), channel_id=1, source_target_pairs={{0,2},{1,3},{2,0},{3,1},{4,6},{5,7},{6,4},{7,5}} | collective-permute-start | bytes 1572872 | tf_op jit(solution)/shard_map/ppermute | solution.py:173
  175.0 87.3 %collective-permute-start.2 = (bf16[128,2048]{1,0:T(8,128)(2,1)S(1)}, bf16[128,2048]{1,0:T(8,128)(2,1)}, u32[]{:S(2)}, u32[]{:S(2)}) collective-permute-start(bf16[128,2048]{1,0:T(8,128)(2,1)S(1)} %maximum_select_fusion.refs_0_), channel_id=1, source_target_pairs={{0,4},{1,5},{2,6},{3,7},{4,0},{5,1},{6,2},{7,3}} | collective-permute-start | bytes 1572872 | tf_op jit(solution)/shard_map/ppermute | solution.py:173
  183.2 79.1 %collective-permute-start.3 = (bf16[128,2048]{1,0:T(8,128)(2,1)S(1)}, bf16[128,2048]{1,0:T(8,128)(2,1)}, u32[]{:S(2)}, u32[]{:S(2)}) collective-permute-start(bf16[128,2048]{1,0:T(8,128)(2,1)S(1)} %maximum_select_fusion.refs_0_), channel_id=1, source_target_pairs={{0,6},{1,7},{2,4},{3,5},{4,2},{5,3},{6,0},{7,1}} | collective-permute-start | bytes 1572872 | tf_op jit(solution)/shard_map/ppermute | solution.py:173
  192.1 33.5 %collective-permute-start.16 = (bf16[512,640]{1,0:T(8,128)(2,1)}, bf16[512,640]{1,0:T(8,128)(2,1)}, u32[]{:S(2)}, u32[]{:S(2)}) collective-permute-start(bf16[512,640]{1,0:T(8,128)(2,1)} %get-tuple-element.18), channel_id=1, source_target_pairs={{0,1},{1,0},{2,3},{3,2},{4,5},{5,4},{6,7},{7,6},{8,9},{9,8},{10,11... | collective-permute-start | bytes 1966088 | tf_op jit(solution)/shard_map/ppermute | solution.py:173
  198.5 26.9 %all-to-all-start.3 = ((bf16[8,4,512]{2,1,0:T(4,128)(2,1)}), bf16[8,4,512]{2,1,0:T(4,128)(2,1)S(1)}, u32[]{:S(2)}, u32[]{:S(2)}) async-start(bf16[8,4,512]{2,1,0:T(4,128)(2,1)} %broadcast_in_dim.64), calls=%async_computation.3 | async-start | bytes 65536 | tf_op jit(solution)/shard_map/all_to_all | solution.py:284
  232.9 29.4 %collective-permute-start.18 = (bf16[512,512]{1,0:T(8,128)(2,1)}, bf16[512,512]{1,0:T(8,128)(2,1)}, u32[]{:S(2)}, u32[]{:S(2)}) collective-permute-start(bf16[512,512]{1,0:T(8,128)(2,1)} %collective-permute-done.17.refs_4_), channel_id=1, source_target_pairs={{8,10},{9,11},{10,8},{11,9},{12,14},{13,15},{14,12},{15,13},{16,18... | collective-permute-start | bytes 1572872 | tf_op jit(solution)/shard_map/ppermute | solution.py:173
  234.3 28.0 %collective-permute-start.19 = (bf16[512,512]{1,0:T(8,128)(2,1)}, bf16[512,512]{1,0:T(8,128)(2,1)}, u32[]{:S(2)}, u32[]{:S(2)}) collective-permute-start(bf16[512,512]{1,0:T(8,128)(2,1)} %collective-permute-done.17.refs_4_), channel_id=1, source_target_pairs={{8,12},{9,13},{10,14},{11,15},{12,8},{13,9},{14,10},{15,11},{16,20... | collective-permute-start | bytes 1572872 | tf_op jit(solution)/shard_map/ppermute | solution.py:173
  235.8 26.5 %collective-permute-start.20 = (bf16[512,512]{1,0:T(8,128)(2,1)}, bf16[512,512]{1,0:T(8,128)(2,1)}, u32[]{:S(2)}, u32[]{:S(2)}) collective-permute-start(bf16[512,512]{1,0:T(8,128)(2,1)} %collective-permute-done.17.refs_4_), channel_id=1, source_target_pairs={{8,14},{9,15},{10,12},{11,13},{12,10},{13,11},{14,8},{15,9},{16,22... | collective-permute-start | bytes 1572872 | tf_op jit(solution)/shard_map/ppermute | solution.py:173
  257.2 16.5 %all-to-all-start.4 = ((bf16[8,12,512]{2,1,0:T(8,128)(2,1)}), bf16[8,12,512]{2,1,0:T(8,128)(2,1)}, u32[]{:S(2)}, u32[]{:S(2)}) async-start(bf16[8,12,512]{2,1,0:T(8,128)(2,1)} %broadcast_in_dim.104), calls=%async_computation.4 | async-start | bytes 262144 | tf_op jit(solution)/shard_map/all_to_all | solution.py:284
  287.1 27.4 %all-to-all-start = ((bf16[8,64,512]{2,1,0:T(8,128)(2,1)}), bf16[8,64,512]{2,1,0:T(8,128)(2,1)S(1)}, u32[]{:S(2)}, u32[]{:S(2)}) async-start(bf16[8,64,512]{2,1,0:T(8,128)(2,1)} %bitcast.8), calls=%async_computation | async-start | bytes 1048576 | tf_op jit(solution)/shard_map/all_to_all | solution.py:279
  314.5 21.0 %all-to-all-start.5 = ((bf16[8,8,4096]{2,1,0:T(8,128)(2,1)}), bf16[8,8,4096]{2,1,0:T(8,128)(2,1)S(1)}, u32[]{:S(2)}, u32[]{:S(2)}) async-start(bf16[8,8,4096]{2,1,0:T(8,128)(2,1)} %fusion.1), calls=%async_computation.5 | async-start | bytes 1048576 | tf_op jit(solution)/shard_map/all_to_all | solution.py:343
  320.7 16.5 %collective-permute-start.22 = (bf16[64,4096]{1,0:T(8,128)(2,1)S(1)}, bf16[64,4096]{1,0:T(8,128)(2,1)S(1)}, u32[]{:S(2)}, u32[]{:S(2)}) collective-permute-start(bf16[64,4096]{1,0:T(8,128)(2,1)S(1)} %bitcast.91), channel_id=1, source_target_pairs={{0,8},{1,9},{2,10},{3,11},{4,12},{5,13},{6,14},{7,15},{8,16},{9,17... | collective-permute-start | bytes 1572872 | tf_op jit(solution)/shard_map/ppermute | solution.py:173
  (29 other events, 332.5 us)

commit v3 on v2

--- a/solution.py
+++ b/solution.py
@@ -208,6 +208,12 @@
         even, odd = jnp.concatenate(pieces[0::2], axis=1), jnp.concatenate(pieces[1::2], axis=1)
         return jnp.where(side == 0, even, odd), jnp.where(side == 0, odd, even)
 
+    def fan(x, pairs, steps):
+        got = {}
+        for k in sorted(steps, key=lambda k: (k != half // 2, k == 0, k)):
+            got[k] = send(x, [(a, b, 2 * k) for a, b in pairs])
+        return [got[k] for k in steps]
+
     def gathered(x, owners):
         here, leave = sides(x)
         there = send(leave, [(a, a, 1) for a in owners])
@@ -216,7 +222,7 @@
             jnp.concatenate([here, there], axis=0),
             jnp.concatenate([there, here], axis=0),
         )
-        return [pair] + [send(pair, [(a, a, 2 * k) for a in owners]) for k in range(1, half)]
+        return [pair] + fan(pair, [(a, a) for a in owners], range(1, half))
 
     entry = jnp.where(section == helper, fresh_batches[0], held_states[0])
     entry_piles = gathered(entry, used)
@@ -258,16 +264,10 @@
     for tick in range(1, TICKS):
         top = last_full + tick
         if tick == 1:
-            piles = [
-                send(block, [(a - 1, a, 2 * k) for a in range(1, top + 1)])
-                for k in range(half)
-            ]
+            piles = fan(block, [(a - 1, a) for a in range(1, top + 1)], range(half))
         else:
             block = send(block, [(a - 1, a, 0) for a in range(1, top + 1)])
-            piles = [block] + [
-                send(block, [(a, a, 2 * k) for a in range(1, top + 1)])
-                for k in range(1, half)
-            ]
+            piles = [block] + fan(block, [(a, a) for a in range(1, top + 1)], range(1, half))
         block, _ = layer(
             fresh_piles[tick - 1],
             piles,

time: 341 us -> 341 us (level)
  no operation moved by 1% of the time
where the time goes in v3:
time: 341 us; the launch traced here: 339 us
  starting transfers between devices  122 us (36%)
  waiting for transfers between devices  75.8 us (22%)
  blocking collectives  61.3 us (18%)
  Pallas kernels  31.2 us (9%)
  other arithmetic  21.6 us (6%)
  local copies, waits for them, and re-layouts  17.4 us (5%)
  matrix products  8.79 us (3%)
    ppermute x25, starting transfers between devices, send(): lax.ppermute(x, AXES, [(a * dps + i, b * dps + (i ^ flip)) for a, b, flip...  69.5 us
    ppermute x25, waiting for transfers between devices, send(): lax.ppermute(x, AXES, [(a * dps + i, b * dps + (i ^ flip)) for a, b, flip...  56.8 us
    all_to_all x3, starting transfers between devices, spread(): lax.all_to_all(jnp.broadcast_to(x[None], (dps, *x.shape)), 'dp', split_ax...  34.2 us
    all_gather x1, blocking collectives, on_device(): owner_queries = lax.all_gather(queries, 'section', axis=0, tiled=True)  27.3 us
    all_gather x1, blocking collectives, on_device(): lax.all_gather(jnp.concatenate(exits, axis=0), 'section', axis=0)  19.3 us
    all_gather x1, blocking collectives, on_device(): owner_grads = lax.all_gather(row_grad, 'section', axis=0, tiled=True)  14.7 us
    pallas_call x3, Pallas kernels, sent_half(): pl.pallas_call(functools.partial(sent_kernel, len(row_piles)), out_shape=...  12.5 us
    all_to_all x1, waiting for transfers between devices, on_device(): lax.all_to_all(received_grad, 'dp', split_axis=0, concat_axis=0, tiled=True)  11.8 us
  transfers between devices with their start and end apart: 31, of which 9 were waited for; matrix products, arithmetic and copies ran while one was open for 11% of the time, Pallas kernels for 7%

profile of v3, /device:TPU:0, one launch (start us, length us, event | category | flops | bytes accessed | tf_op | source)
XLA Modules:
  0.0 339.1 jit_solution(9276298148253023953)
XLA Ops:
  1.2 5.0 %shard_map.129 = bf16[2048,512]{1,0:T(8,128)(2,1)} custom-call(s32[4]{0:T(128)} %add_subtract_fusion.at_ref, bf16[4096,512]{1,0:T(8,128)(2,1)} %bitcast.84, f32[8,1,512]{2,1,0:T(1,128)} %bitcast.92), custom_call_target="tpu_custom_call" | custom-call | flops 1048576 | bytes 4194304 | tf_op jit(solution)/shard_map/pallas_call | solution.py:33
  6.2 4.9 %collective-permute-start.8 = (bf16[2048,512]{1,0:T(8,128)(2,1)}, bf16[2048,512]{1,0:T(8,128)(2,1)S(1)}, u32[]{:S(2)}, u32[]{:S(2)}) collective-permute-start(bf16[2048,512]{1,0:T(8,128)(2,1)} %shard_map.129), channel_id=1, source_target_pairs={{0,1},{1,0},{2,3},{3,2},{4,5},{5,4},{6,7},{7,6}} | collective-permute-start | bytes 6291464 | tf_op jit(solution)/shard_map/ppermute | solution.py:173
  16.0 4.9 %all-to-all-start.1 = ((bf16[8,8,4736]{2,1,0:T(8,128)(2,1)}), bf16[8,8,4736]{2,1,0:T(8,128)(2,1)}, u32[]{:S(2)}, u32[]{:S(2)}) async-start(bf16[8,8,4736]{2,1,0:T(8,128)(2,1)} %pad_maximum_fusion), calls=%async_computation.1 | async-start | bytes 1212416 | tf_op jit(solution)/shard_map/all_to_all | solution.py:244
  33.3 33.7 %collective-permute-done.4 = bf16[64,2048]{1,0:T(8,128)(2,1)S(1)} collective-permute-done((bf16[64,2048]{1,0:T(8,128)(2,1)S(1)}, bf16[64,2048]{1,0:T(8,128)(2,1)S(1)}, u32[]{:S(2)}, u32[]{:S(2)}) %collective-permute-start.4) | collective-permute-done | bytes 262176 | tf_op jit(solution)/shard_map/ppermute | solution.py:173
  72.6 4.5 %collective-permute-start.6 = (bf16[128,2048]{1,0:T(8,128)(2,1)S(1)}, bf16[128,2048]{1,0:T(8,128)(2,1)}, u32[]{:S(2)}, u32[]{:S(2)}) collective-permute-start(bf16[128,2048]{1,0:T(8,128)(2,1)S(1)} %maximum_select_fusion.1.refs_0_), channel_id=1, source_target_pairs={{0,4},{1,5},{2,6},{3,7},{4,0},{5,1},{6,2},{7,3},{16,20},{17,21},{1... | collective-permute-start | bytes 1572872 | tf_op jit(solution)/shard_map/ppermute | solution.py:173
  87.3 8.7 %collective-permute-done.6.refs_2_ = bf16[128,2048]{1,0:T(8,128)(2,1)} collective-permute-done((bf16[128,2048]{1,0:T(8,128)(2,1)S(1)}, bf16[128,2048]{1,0:T(8,128)(2,1)}, u32[]{:S(2)}, u32[]{:S(2)}) %collective-permute-start.6) | collective-permute-done | bytes 524320 | tf_op jit(solution)/shard_map/ppermute | solution.py:173
  104.2 27.3 %all_gather.15 = bf16[32,4096]{1,0:T(8,128)(2,1)} all-gather(bf16[8,4096]{1,0:T(8,128)(2,1)S(1)} %copy-done.14), channel_id=1, replica_groups=mesh['section'=4,'dp'=8] {'section'}, dimensions={0}, use_global_device_ids=true | all-gather | bytes 327680 | tf_op jit(solution)/shard_map/all_gather | solution.py:245
  132.7 4.9 %shard_map.131.weight_ref = bf16[2048,512]{1,0:T(8,128)(2,1)} custom-call(s32[4]{0:T(128)} %fusion.25.at_ref, bf16[4096,512]{1,0:T(8,128)(2,1)} %bitcast.85, f32[8,1,512]{2,1,0:T(1,128)} %bitcast.93), custom_call_target="tpu_custom_call" | custom-call | flops 1048576 | bytes 4194304 | tf_op jit(solution)/shard_map/pallas_call | solution.py:33
  138.2 9.4 %all-to-all-start.2 = ((bf16[8,4,512]{2,1,0:T(4,128)(2,1)}), bf16[8,4,512]{2,1,0:T(4,128)(2,1)S(1)}, u32[]{:S(2)}, u32[]{:S(2)}) async-start(bf16[8,4,512]{2,1,0:T(4,128)(2,1)} %broadcast_in_dim.63), calls=%async_computation.2 | async-start | bytes 65536 | tf_op jit(solution)/shard_map/all_to_all | solution.py:284
  154.6 5.8 %collective-permute-done.10.other_ref = bf16[512,640]{1,0:T(8,128)(2,1)} collective-permute-done((bf16[512,640]{1,0:T(8,128)(2,1)}, bf16[512,640]{1,0:T(8,128)(2,1)}, u32[]{:S(2)}, u32[]{:S(2)}) %collective-permute-start.10) | collective-permute-done | bytes 655392 | tf_op jit(solution)/shard_map/ppermute | solution.py:173
  170.9 4.1 %collective-permute-start.1 = (bf16[128,2048]{1,0:T(8,128)(2,1)S(1)}, bf16[128,2048]{1,0:T(8,128)(2,1)}, u32[]{:S(2)}, u32[]{:S(2)}) collective-permute-start(bf16[128,2048]{1,0:T(8,128)(2,1)S(1)} %maximum_select_fusion.refs_0_), channel_id=1, source_target_pairs={{0,2},{1,3},{2,0},{3,1},{4,6},{5,7},{6,4},{7,5}} | collective-permute-start | bytes 1572872 | tf_op jit(solution)/shard_map/ppermute | solution.py:173
  175.0 8.2 %collective-permute-start.2 = (bf16[128,2048]{1,0:T(8,128)(2,1)S(1)}, bf16[128,2048]{1,0:T(8,128)(2,1)}, u32[]{:S(2)}, u32[]{:S(2)}) collective-permute-start(bf16[128,2048]{1,0:T(8,128)(2,1)S(1)} %maximum_select_fusion.refs_0_), channel_id=1, source_target_pairs={{0,4},{1,5},{2,6},{3,7},{4,0},{5,1},{6,2},{7,3}} | collective-permute-start | bytes 1572872 | tf_op jit(solution)/shard_map/ppermute | solution.py:173
  183.2 4.8 %collective-permute-start.3 = (bf16[128,2048]{1,0:T(8,128)(2,1)S(1)}, bf16[128,2048]{1,0:T(8,128)(2,1)}, u32[]{:S(2)}, u32[]{:S(2)}) collective-permute-start(bf16[128,2048]{1,0:T(8,128)(2,1)S(1)} %maximum_select_fusion.refs_0_), channel_id=1, source_target_pairs={{0,6},{1,7},{2,4},{3,5},{4,2},{5,3},{6,0},{7,1}} | collective-permute-start | bytes 1572872 | tf_op jit(solution)/shard_map/ppermute | solution.py:173
  188.0 4.1 %shard_map.133 = (bf16[512,640]{1,0:T(8,128)(2,1)}, f32[512,128]{1,0:T(8,128)S(1)}, bf16[512,2048]{1,0:T(8,128)(2,1)S(1)}) custom-call(s32[3]{0:T(128)S(1)} %pad_add_fusion.at_ref, bf16[512,2048]{1,0:T(8,128)(2,1)} %collective-permute-done.9.refs_0_, bf16[512,512]{1,0:T(8,128)(2,1)S(1)} %collective-permute-done.11.refs_1_, ...), custom_call_target="tpu_custom_call" | custom-call | flops 1073741824 | bytes 4194304 | tf_op jit(solution)/shard_map/pallas_call | solution.py:121
  198.5 20.2 %all-to-all-start.3 = ((bf16[8,4,512]{2,1,0:T(4,128)(2,1)}), bf16[8,4,512]{2,1,0:T(4,128)(2,1)S(1)}, u32[]{:S(2)}, u32[]{:S(2)}) async-start(bf16[8,4,512]{2,1,0:T(4,128)(2,1)} %broadcast_in_dim.64), calls=%async_computation.3 | async-start | bytes 65536 | tf_op jit(solution)/shard_map/all_to_all | solution.py:284
  219.8 5.7 %all-to-all-done.3 = bf16[8,4,512]{2,1,0:T(4,128)(2,1)S(1)} async-done(((bf16[8,4,512]{2,1,0:T(4,128)(2,1)}), bf16[8,4,512]{2,1,0:T(4,128)(2,1)S(1)}, u32[]{:S(2)}, u32[]{:S(2)}) %all-to-all-start.3) | async-done | bytes 32800 | tf_op jit(solution)/shard_map/all_to_all | solution.py:284
  237.3 19.3 %all-gather.1 = bf16[4,12,512]{2,1,0:T(8,128)(2,1)S(1)} all-gather(bf16[1,12,512]{2,1,0:T(8,128)(2,1)S(1)} %maximum_bitcast_fusion), channel_id=2, replica_groups=mesh['section'=4,'dp'=8] {'section'}, dimensions={0}, use_global_device_ids=true | all-gather | bytes 61440 | tf_op jit(solution)/shard_map/all_gather | solution.py:307
  257.2 4.5 %all-to-all-start.4 = ((bf16[8,12,512]{2,1,0:T(8,128)(2,1)}), bf16[8,12,512]{2,1,0:T(8,128)(2,1)}, u32[]{:S(2)}, u32[]{:S(2)}) async-start(bf16[8,12,512]{2,1,0:T(8,128)(2,1)} %broadcast_in_dim.104), calls=%async_computation.4 | async-start | bytes 262144 | tf_op jit(solution)/shard_map/all_to_all | solution.py:284
  263.9 4.5 %shard_map.135 = (bf16[512,640]{1,0:T(8,128)(2,1)}, f32[512,128]{1,0:T(8,128)S(1)}, bf16[512,2048]{1,0:T(8,128)(2,1)S(1)}) custom-call(s32[3]{0:T(128)S(1)} %pad_add_fusion.at_ref, bf16[128,2048]{1,0:T(8,128)(2,1)S(1)} %maximum_select_fusion.refs_0_, bf16[128,2048]{1,0:T(8,128)(2,1)} %collective-permute-done.1.refs_1_, ...), custom_call_target="tpu_custom_call" | custom-call | flops 1073741824 | bytes 4194304 | tf_op jit(solution)/shard_map/pallas_call | solution.py:121
  278.4 5.9 %collective-permute-done.21.other_ref = bf16[512,640]{1,0:T(8,128)(2,1)S(1)} collective-permute-done((bf16[512,640]{1,0:T(8,128)(2,1)}, bf16[512,640]{1,0:T(8,128)(2,1)S(1)}, u32[]{:S(2)}, u32[]{:S(2)}) %collective-permute-start.21) | collective-permute-done | bytes 655392 | tf_op jit(solution)/shard_map/ppermute | solution.py:173
  287.1 7.2 %all-to-all-start = ((bf16[8,64,512]{2,1,0:T(8,128)(2,1)}), bf16[8,64,512]{2,1,0:T(8,128)(2,1)S(1)}, u32[]{:S(2)}, u32[]{:S(2)}) async-start(bf16[8,64,512]{2,1,0:T(8,128)(2,1)} %bitcast.8), calls=%async_computation | async-start | bytes 1048576 | tf_op jit(solution)/shard_map/all_to_all | solution.py:279
  297.5 14.7 %all_gather.14 = f32[32,64]{1,0:T(8,128)S(1)} all-gather(f32[8,64]{1,0:T(8,128)S(1)} %select_reduce_fusion), channel_id=1, replica_groups=mesh['section'=4,'dp'=8] {'section'}, dimensions={0}, use_global_device_ids=true | all-gather | bytes 10240 | tf_op jit(solution)/shard_map/all_gather | solution.py:338
  314.5 6.0 %all-to-all-start.5 = ((bf16[8,8,4096]{2,1,0:T(8,128)(2,1)}), bf16[8,8,4096]{2,1,0:T(8,128)(2,1)S(1)}, u32[]{:S(2)}, u32[]{:S(2)}) async-start(bf16[8,8,4096]{2,1,0:T(8,128)(2,1)} %fusion.1), calls=%async_computation.5 | async-start | bytes 1048576 | tf_op jit(solution)/shard_map/all_to_all | solution.py:343
  323.7 11.8 %all-to-all-done.5 = bf16[8,8,4096]{2,1,0:T(8,128)(2,1)S(1)} async-done(((bf16[8,8,4096]{2,1,0:T(8,128)(2,1)}), bf16[8,8,4096]{2,1,0:T(8,128)(2,1)S(1)}, u32[]{:S(2)}, u32[]{:S(2)}) %all-to-all-start.5) | async-done | bytes 524320 | tf_op jit(solution)/shard_map/all_to_all | solution.py:343
  (170 shorter events, 107.7 us)
Async XLA Ops:
  6.2 89.8 %collective-permute-start.8 = (bf16[2048,512]{1,0:T(8,128)(2,1)}, bf16[2048,512]{1,0:T(8,128)(2,1)S(1)}, u32[]{:S(2)}, u32[]{:S(2)}) collective-permute-start(bf16[2048,512]{1,0:T(8,128)(2,1)} %shard_map.129), channel_id=1, source_target_pairs={{0,1},{1,0},{2,3},{3,2},{4,5},{5,4},{6,7},{7,6}} | collective-permute-start | bytes 6291464 | tf_op jit(solution)/shard_map/ppermute | solution.py:173
  11.1 158.2 %collective-permute-start.15 = (bf16[2048,512]{1,0:T(8,128)(2,1)}, bf16[2048,512]{1,0:T(8,128)(2,1)}, u32[]{:S(2)}, u32[]{:S(2)}) collective-permute-start(bf16[2048,512]{1,0:T(8,128)(2,1)} %shard_map.129), channel_id=1, source_target_pairs={{8,9},{9,8},{10,11},{11,10},{12,13},{13,12},{14,15},{15,14},{16,17... | collective-permute-start | bytes 6291464 | tf_op jit(solution)/shard_map/ppermute | solution.py:173
  16.0 63.0 %all-to-all-start.1 = ((bf16[8,8,4736]{2,1,0:T(8,128)(2,1)}), bf16[8,8,4736]{2,1,0:T(8,128)(2,1)}, u32[]{:S(2)}, u32[]{:S(2)}) async-start(bf16[8,8,4736]{2,1,0:T(8,128)(2,1)} %pad_maximum_fusion), calls=%async_computation.1 | async-start | bytes 1212416 | tf_op jit(solution)/shard_map/all_to_all | solution.py:244
  25.1 41.9 %collective-permute-start.4 = (bf16[64,2048]{1,0:T(8,128)(2,1)S(1)}, bf16[64,2048]{1,0:T(8,128)(2,1)S(1)}, u32[]{:S(2)}, u32[]{:S(2)}) collective-permute-start(bf16[64,2048]{1,0:T(8,128)(2,1)S(1)} %get-tuple-element.28), channel_id=1, source_target_pairs={{0,1},{1,0},{2,3},{3,2},{4,5},{5,4},{6,7},{7,6},{16,17},{17,16},{1... | collective-permute-start | bytes 786440 | tf_op jit(solution)/shard_map/ppermute | solution.py:173
  72.6 23.4 %collective-permute-start.6 = (bf16[128,2048]{1,0:T(8,128)(2,1)S(1)}, bf16[128,2048]{1,0:T(8,128)(2,1)}, u32[]{:S(2)}, u32[]{:S(2)}) collective-permute-start(bf16[128,2048]{1,0:T(8,128)(2,1)S(1)} %maximum_select_fusion.1.refs_0_), channel_id=1, source_target_pairs={{0,4},{1,5},{2,6},{3,7},{4,0},{5,1},{6,2},{7,3},{16,20},{17,21},{1... | collective-permute-start | bytes 1572872 | tf_op jit(solution)/shard_map/ppermute | solution.py:173
  77.1 18.9 %collective-permute-start.7 = (bf16[128,2048]{1,0:T(8,128)(2,1)S(1)}, bf16[128,2048]{1,0:T(8,128)(2,1)}, u32[]{:S(2)}, u32[]{:S(2)}) collective-permute-start(bf16[128,2048]{1,0:T(8,128)(2,1)S(1)} %maximum_select_fusion.1.refs_0_), channel_id=1, source_target_pairs={{0,6},{1,7},{2,4},{3,5},{4,2},{5,3},{6,0},{7,1},{16,22},{17,23},{1... | collective-permute-start | bytes 1572872 | tf_op jit(solution)/shard_map/ppermute | solution.py:173
  83.4 68.1 %collective-permute-start = (bf16[64,2048]{1,0:T(8,128)(2,1)}, bf16[64,2048]{1,0:T(8,128)(2,1)}, u32[]{:S(2)}, u32[]{:S(2)}) collective-permute-start(bf16[64,2048]{1,0:T(8,128)(2,1)} %get-tuple-element.38), channel_id=1, source_target_pairs={{0,1},{1,0},{2,3},{3,2},{4,5},{5,4},{6,7},{7,6}} | collective-permute-start | bytes 786440 | tf_op jit(solution)/shard_map/ppermute | solution.py:173
  100.7 87.3 %collective-permute-start.9 = (bf16[512,2048]{1,0:T(8,128)(2,1)}, bf16[512,2048]{1,0:T(8,128)(2,1)}, u32[]{:S(2)}, u32[]{:S(2)}) collective-permute-start(bf16[512,2048]{1,0:T(8,128)(2,1)} %get-tuple-element.14.states_ref), channel_id=1, source_target_pairs={{16,0},{17,1},{18,2},{19,3},{20,4},{21,5},{22,6},{23,7}} | collective-permute-start | bytes 6291464 | tf_op jit(solution)/shard_map/ppermute | solution.py:173
  103.5 34.0 %collective-permute-start.23 = (bf16[4,512]{1,0:T(4,128)(2,1)S(1)}, bf16[4,512]{1,0:T(4,128)(2,1)S(1)}, u32[]{:S(2)}, u32[]{:S(2)}) collective-permute-start(bf16[4,512]{1,0:T(4,128)(2,1)S(1)} %fusion.20), channel_id=1, source_target_pairs={{8,16},{9,17},{10,18},{11,19},{12,20},{13,21},{14,22},{15,23},{16,... | collective-permute-start | bytes 12296 | tf_op jit(solution)/shard_map/ppermute | solution.py:173
  138.2 16.2 %all-to-all-start.2 = ((bf16[8,4,512]{2,1,0:T(4,128)(2,1)}), bf16[8,4,512]{2,1,0:T(4,128)(2,1)S(1)}, u32[]{:S(2)}, u32[]{:S(2)}) async-start(bf16[8,4,512]{2,1,0:T(4,128)(2,1)} %broadcast_in_dim.63), calls=%async_computation.2 | async-start | bytes 65536 | tf_op jit(solution)/shard_map/all_to_all | solution.py:284
  167.9 15.3 %collective-permute-start.13 = (bf16[512,512]{1,0:T(8,128)(2,1)S(1)}, bf16[512,512]{1,0:T(8,128)(2,1)S(1)}, u32[]{:S(2)}, u32[]{:S(2)}) collective-permute-start(bf16[512,512]{1,0:T(8,128)(2,1)S(1)} %shard_map.132), channel_id=1, source_target_pairs={{0,12},{1,13},{2,14},{3,15},{4,8},{5,9},{6,10},{7,11}} | collective-permute-start | bytes 1572872 | tf_op jit(solution)/shard_map/ppermute | solution.py:173
  169.3 18.7 %collective-permute-start.14 = (bf16[512,512]{1,0:T(8,128)(2,1)S(1)}, bf16[512,512]{1,0:T(8,128)(2,1)S(1)}, u32[]{:S(2)}, u32[]{:S(2)}) collective-permute-start(bf16[512,512]{1,0:T(8,128)(2,1)S(1)} %shard_map.132), channel_id=1, source_target_pairs={{0,14},{1,15},{2,12},{3,13},{4,10},{5,11},{6,8},{7,9}} | collective-permute-start | bytes 1572872 | tf_op jit(solution)/shard_map/ppermute | solution.py:173
  170.9 64.9 %collective-permute-start.1 = (bf16[128,2048]{1,0:T(8,128)(2,1)S(1)}, bf16[128,2048]{1,0:T(8,128)(2,1)}, u32[]{:S(2)}, u32[]{:S(2)}) collective-permute-start(bf16[128,2048]{1,0:T(8,128)(2,1)S(1)} %maximum_select_fusion.refs_0_), channel_id=1, source_target_pairs={{0,2},{1,3},{2,0},{3,1},{4,6},{5,7},{6,4},{7,5}} | collective-permute-start | bytes 1572872 | tf_op jit(solution)/shard_map/ppermute | solution.py:173
  175.0 87.3 %collective-permute-start.2 = (bf16[128,2048]{1,0:T(8,128)(2,1)S(1)}, bf16[128,2048]{1,0:T(8,128)(2,1)}, u32[]{:S(2)}, u32[]{:S(2)}) collective-permute-start(bf16[128,2048]{1,0:T(8,128)(2,1)S(1)} %maximum_select_fusion.refs_0_), channel_id=1, source_target_pairs={{0,4},{1,5},{2,6},{3,7},{4,0},{5,1},{6,2},{7,3}} | collective-permute-start | bytes 1572872 | tf_op jit(solution)/shard_map/ppermute | solution.py:173
  183.2 79.1 %collective-permute-start.3 = (bf16[128,2048]{1,0:T(8,128)(2,1)S(1)}, bf16[128,2048]{1,0:T(8,128)(2,1)}, u32[]{:S(2)}, u32[]{:S(2)}) collective-permute-start(bf16[128,2048]{1,0:T(8,128)(2,1)S(1)} %maximum_select_fusion.refs_0_), channel_id=1, source_target_pairs={{0,6},{1,7},{2,4},{3,5},{4,2},{5,3},{6,0},{7,1}} | collective-permute-start | bytes 1572872 | tf_op jit(solution)/shard_map/ppermute | solution.py:173
  192.1 33.5 %collective-permute-start.16 = (bf16[512,640]{1,0:T(8,128)(2,1)}, bf16[512,640]{1,0:T(8,128)(2,1)}, u32[]{:S(2)}, u32[]{:S(2)}) collective-permute-start(bf16[512,640]{1,0:T(8,128)(2,1)} %get-tuple-element.18), channel_id=1, source_target_pairs={{0,1},{1,0},{2,3},{3,2},{4,5},{5,4},{6,7},{7,6},{8,9},{9,8},{10,11... | collective-permute-start | bytes 1966088 | tf_op jit(solution)/shard_map/ppermute | solution.py:173
  198.5 26.9 %all-to-all-start.3 = ((bf16[8,4,512]{2,1,0:T(4,128)(2,1)}), bf16[8,4,512]{2,1,0:T(4,128)(2,1)S(1)}, u32[]{:S(2)}, u32[]{:S(2)}) async-start(bf16[8,4,512]{2,1,0:T(4,128)(2,1)} %broadcast_in_dim.64), calls=%async_computation.3 | async-start | bytes 65536 | tf_op jit(solution)/shard_map/all_to_all | solution.py:284
  232.9 29.4 %collective-permute-start.18 = (bf16[512,512]{1,0:T(8,128)(2,1)}, bf16[512,512]{1,0:T(8,128)(2,1)}, u32[]{:S(2)}, u32[]{:S(2)}) collective-permute-start(bf16[512,512]{1,0:T(8,128)(2,1)} %collective-permute-done.17.refs_4_), channel_id=1, source_target_pairs={{8,10},{9,11},{10,8},{11,9},{12,14},{13,15},{14,12},{15,13},{16,18... | collective-permute-start | bytes 1572872 | tf_op jit(solution)/shard_map/ppermute | solution.py:173
  234.3 28.0 %collective-permute-start.19 = (bf16[512,512]{1,0:T(8,128)(2,1)}, bf16[512,512]{1,0:T(8,128)(2,1)}, u32[]{:S(2)}, u32[]{:S(2)}) collective-permute-start(bf16[512,512]{1,0:T(8,128)(2,1)} %collective-permute-done.17.refs_4_), channel_id=1, source_target_pairs={{8,12},{9,13},{10,14},{11,15},{12,8},{13,9},{14,10},{15,11},{16,20... | collective-permute-start | bytes 1572872 | tf_op jit(solution)/shard_map/ppermute | solution.py:173
  235.8 26.5 %collective-permute-start.20 = (bf16[512,512]{1,0:T(8,128)(2,1)}, bf16[512,512]{1,0:T(8,128)(2,1)}, u32[]{:S(2)}, u32[]{:S(2)}) collective-permute-start(bf16[512,512]{1,0:T(8,128)(2,1)} %collective-permute-done.17.refs_4_), channel_id=1, source_target_pairs={{8,14},{9,15},{10,12},{11,13},{12,10},{13,11},{14,8},{15,9},{16,22... | collective-permute-start | bytes 1572872 | tf_op jit(solution)/shard_map/ppermute | solution.py:173
  257.2 16.5 %all-to-all-start.4 = ((bf16[8,12,512]{2,1,0:T(8,128)(2,1)}), bf16[8,12,512]{2,1,0:T(8,128)(2,1)}, u32[]{:S(2)}, u32[]{:S(2)}) async-start(bf16[8,12,512]{2,1,0:T(8,128)(2,1)} %broadcast_in_dim.104), calls=%async_computation.4 | async-start | bytes 262144 | tf_op jit(solution)/shard_map/all_to_all | solution.py:284
  287.1 27.4 %all-to-all-start = ((bf16[8,64,512]{2,1,0:T(8,128)(2,1)}), bf16[8,64,512]{2,1,0:T(8,128)(2,1)S(1)}, u32[]{:S(2)}, u32[]{:S(2)}) async-start(bf16[8,64,512]{2,1,0:T(8,128)(2,1)} %bitcast.8), calls=%async_computation | async-start | bytes 1048576 | tf_op jit(solution)/shard_map/all_to_all | solution.py:279
  314.5 21.0 %all-to-all-start.5 = ((bf16[8,8,4096]{2,1,0:T(8,128)(2,1)}), bf16[8,8,4096]{2,1,0:T(8,128)(2,1)S(1)}, u32[]{:S(2)}, u32[]{:S(2)}) async-start(bf16[8,8,4096]{2,1,0:T(8,128)(2,1)} %fusion.1), calls=%async_computation.5 | async-start | bytes 1048576 | tf_op jit(solution)/shard_map/all_to_all | solution.py:343
  320.7 16.5 %collective-permute-start.22 = (bf16[64,4096]{1,0:T(8,128)(2,1)S(1)}, bf16[64,4096]{1,0:T(8,128)(2,1)S(1)}, u32[]{:S(2)}, u32[]{:S(2)}) collective-permute-start(bf16[64,4096]{1,0:T(8,128)(2,1)S(1)} %bitcast.91), channel_id=1, source_target_pairs={{0,8},{1,9},{2,10},{3,11},{4,12},{5,13},{6,14},{7,15},{8,16},{9,17... | collective-permute-start | bytes 1572872 | tf_op jit(solution)/shard_map/ppermute | solution.py:173
  (29 other events, 332.5 us)
